TPU v7x, 32 devices: a whole 2x2x4 slice. The times are simulated.
32 devices in a mesh: fsdp: 2 (over core), ctx: 8 (over z, y), tp: 2 (over x).
Axes of the slice: x: 2, y: 2, z: 4, core: 2. Of those that a mesh axis runs over, the one named last changes fastest.
Arguments:
- tokens: bfloat16 [2, 2048, 512], P('fsdp', 'ctx'), may hold values from -11 to 11
- source_states: bfloat16 [2, 1024, 512], P('fsdp', 'ctx'), may hold values from -6 to 6
- block_ids: int32 [2, 2048], P('fsdp', 'ctx'), may hold values from 0 to 15, never falling along the last dimension, each value on 1 to 256 neighbouring positions
- source_len: int32 [2], P('fsdp'), may hold values from 256 to 1024, as said below
- out_grad: bfloat16 [2, 2048, 512], P('fsdp', 'ctx'), may hold values from -6 to 6
- self_qkv: bfloat16 [3, 512, 512], P(None, 'fsdp', 'tp'), may hold values from -0.25 to 0.25
- self_out: bfloat16 [512, 512], P('tp', 'fsdp'), may hold values from -0.75 to 0.75
- cross_q: bfloat16 [512, 512], P('fsdp', 'tp'), may hold values from -0.25 to 0.25
- cross_kv: bfloat16 [2, 512, 512], P(None, 'fsdp', 'tp'), may hold values from -0.25 to 0.25
- cross_out: bfloat16 [512, 512], P('tp', 'fsdp'), may hold values from -1 to 1
- ffn_in: bfloat16 [512, 2048], P('fsdp', 'tp'), may hold values from -0.25 to 0.25
- ffn_out: bfloat16 [2048, 512], P('tp', 'fsdp'), may hold values from -0.125 to 0.125
- attn_bias: float32 [4, 512], P('fsdp', 'tp'), may hold values from -3 to 3
- ffn_in_bias: float32 [2048], P('tp'), may hold values from -3 to 3
- out_bias: float32 [3, 512], P(None, 'fsdp'), may hold values from -2 to 2
- norm_gain: float32 [3, 512], P(None, 'fsdp'), may hold values from 0.5 to 1.5
- norm_bias: float32 [3, 512], P(None, 'fsdp'), may hold values from -2 to 2
Outputs:
- output: bfloat16 [2, 2048, 512], P('fsdp', 'ctx')
- input_grad: float32 [2, 2048, 512], P('fsdp', 'ctx')
- source_grad: float32 [2, 1024, 512], P('fsdp', 'ctx')
- rms_values: float32 [4], replicated
- grad_self_qkv: float32 [3, 512, 512], P(None, 'fsdp', 'tp')
- grad_self_out: float32 [512, 512], P('tp', 'fsdp')
- grad_cross_q: float32 [512, 512], P('fsdp', 'tp')
- grad_cross_kv: float32 [2, 512, 512], P(None, 'fsdp', 'tp')
- grad_cross_out: float32 [512, 512], P('tp', 'fsdp')
- grad_ffn_in: float32 [512, 2048], P('fsdp', 'tp')
- grad_ffn_out: float32 [2048, 512], P('tp', 'fsdp')
- grad_attn_bias: float32 [4, 512], P('fsdp', 'tp')
- grad_ffn_in_bias: float32 [2048], P('tp')
- grad_out_bias: float32 [3, 512], P(None, 'fsdp')
- grad_norm_gain: float32 [3, 512], P(None, 'fsdp')
- grad_norm_bias: float32 [3, 512], P(None, 'fsdp')
Inputs may be any that keep to these rules, and one draw needn't show every extreme that they name: `block_ids`: along each sequence the ids never fall; each id covers 1 to 256 consecutive positions, and one covers exactly 256. `source_len`: some sequence uses all 1024 source positions.
All inputs are finite; a program needn't handle non-finite values.
Results may differ from a plain program's by a relative error of at most 0.03.
Values may be sent and summed in bfloat16 or wider, within the bound.
No kernel may reach another device: no remote copies, remote signals or barrier semaphores. Data moves between devices by JAX's collectives and lax.ppermute only.
A program may use at most 128 MiB of HBM per device.

v0:
```python
import jax
import jax.numpy as jnp
from jax import lax
from jax.sharding import PartitionSpec as P

HEAD = 64


NEG = -1e30
EPSILON = 1e-05


def cut_along(x, dim, devices):
    before, after = (x.shape[:dim], x.shape[dim + 1 :])
    return jnp.moveaxis(x.reshape(*before, devices, -1, *after), dim, 0)


def sum_at_owner(x, axis, dim):
    pieces = cut_along(x, dim, lax.axis_size(axis))
    arrived = lax.all_to_all(pieces, axis, split_axis=0, concat_axis=0, tiled=True)
    return arrived.astype(jnp.float32).sum(axis=0)


def in_one_piece(arrays, axis, dim, along):
    both = jnp.concatenate(arrays, axis=along)
    out, at, done = (sum_at_owner(both, axis, dim), 0, [])
    for a in arrays:
        done.append(lax.slice_in_dim(out, at, at + a.shape[along], axis=along))
        at += a.shape[along]
    return tuple(done)


def matmul(left, right):
    return jnp.dot(left, right, preferred_element_type=jnp.float32)


def matmul_tn(left, right):
    return lax.dot_general(
        left, right, (((0,), (0,)), ((), ())), preferred_element_type=jnp.float32
    )


def matmul_nt(left, right):
    return lax.dot_general(
        left, right, (((1,), (1,)), ((), ())), preferred_element_type=jnp.float32
    )


def split_heads(matrix):
    return matrix.reshape(matrix.shape[0], matrix.shape[1] // HEAD, HEAD)


def norm_forward(resid, gain, shift):
    average = jnp.mean(resid, axis=-1, keepdims=True)
    centred = resid - average
    inverse = lax.rsqrt(jnp.mean(centred * centred, axis=-1, keepdims=True) + EPSILON)
    normed = centred * inverse
    return (normed * gain + shift, normed, inverse)


def norm_backward(grad_out, normed, inverse, gain):
    grad_norm = grad_out * gain
    first_mean = jnp.mean(grad_norm, axis=-1, keepdims=True)
    second_mean = jnp.mean(grad_norm * normed, axis=-1, keepdims=True)
    grad_in = inverse * (grad_norm - first_mean - normed * second_mean)
    return (grad_in, jnp.sum(grad_out * normed, axis=0), jnp.sum(grad_out, axis=0))


def in_blocks(items):
    count = items[0].shape[0]
    width = 512
    return tuple((item.reshape((count // width, width) + item.shape[1:]) for item in items))


def pass_state(state):
    return state


def scores_of(query_heads, key_heads, query_segs, key_segs):
    scores = jnp.einsum(
        "qhd,khd->qhk", query_heads, key_heads, preferred_element_type=jnp.float32
    ) * HEAD ** (-0.5)
    allowed = key_segs[None, None, :] <= query_segs[:, None, None]
    return jnp.where(allowed, scores, NEG)


def per_device(
    tokens,
    source_states,
    block_ids,
    source_len,
    out_grad,
    self_qkv,
    self_out,
    cross_q,
    cross_kv,
    cross_out,
    ffn_in,
    ffn_out,
    attn_bias,
    ffn_in_bias,
    out_bias,
    norm_gain,
    norm_bias,
):
    w_qkv, w_out, w_cq, w_ckv, w_co, w_in, w_fout, b_attn, b_out, gains, shifts = (
        lax.all_gather(self_qkv, "fsdp", axis=1, tiled=True),
        lax.all_gather(self_out, "fsdp", axis=1, tiled=True),
        lax.all_gather(cross_q, "fsdp", axis=0, tiled=True),
        lax.all_gather(cross_kv, "fsdp", axis=1, tiled=True),
        lax.all_gather(cross_out, "fsdp", axis=1, tiled=True),
        lax.all_gather(ffn_in, "fsdp", axis=0, tiled=True),
        lax.all_gather(ffn_out, "fsdp", axis=1, tiled=True),
        lax.all_gather(attn_bias.astype(jnp.bfloat16), "fsdp", axis=0, tiled=True).astype(
            attn_bias.dtype
        ),
        lax.all_gather(out_bias.astype(jnp.bfloat16), "fsdp", axis=1, tiled=True).astype(
            out_bias.dtype
        ),
        lax.all_gather(norm_gain.astype(jnp.bfloat16), "fsdp", axis=1, tiled=True).astype(
            norm_gain.dtype
        ),
        lax.all_gather(norm_bias.astype(jnp.bfloat16), "fsdp", axis=1, tiled=True).astype(
            norm_bias.dtype
        ),
    )

    def head_total(partial_value):
        return lax.psum(partial_value.astype(jnp.bfloat16), "tp").astype(jnp.float32)

    inputs = tokens[0]
    resid_in = inputs.astype(jnp.float32)
    query_segs = block_ids[0]
    top_seg = jnp.max(query_segs)
    low_seg = jnp.min(query_segs)
    rows = inputs.shape[0]
    queries = (matmul(inputs, w_qkv[0]) + b_attn[0]).astype(jnp.bfloat16)
    keys = matmul(inputs, w_qkv[1]).astype(jnp.bfloat16)
    values = (matmul(inputs, w_qkv[2]) + b_attn[1]).astype(jnp.bfloat16)
    query_heads = split_heads(queries)
    key_heads = split_heads(keys)
    value_heads = split_heads(values)
    heads = query_heads.shape[1]
    start_state = (jnp.full((rows, heads), NEG, jnp.float32), jnp.zeros((rows, heads), jnp.float32))
    empty_heads = jnp.zeros((rows, heads, HEAD), jnp.float32)

    def stat_one_block(inner, block):

        def stat_compute(current):
            row_max, row_sum = current
            scores = scores_of(query_heads, split_heads(block[0]), query_segs, block[1])
            new_max = jnp.maximum(row_max, jnp.max(scores, axis=-1))
            total = row_sum * jnp.exp(row_max - new_max) + jnp.sum(
                jnp.exp(scores - new_max[..., None]), axis=-1
            )
            return (new_max, total)

        return (lax.cond(jnp.min(block[1]) <= top_seg, stat_compute, pass_state, inner), None)

    row_max, row_sum = lax.scan(
        stat_one_block,
        start_state,
        in_blocks(
            (
                lax.all_gather(keys, "ctx", axis=0, tiled=True),
                lax.all_gather(query_segs, "ctx", axis=0, tiled=True),
            )
        ),
    )[0]
    log_sum = row_max + jnp.log(row_sum)

    def out_one_block(inner, block):

        def out_compute(current):
            scores = scores_of(query_heads, split_heads(block[0]), query_segs, block[2])
            weights = jnp.exp(scores - log_sum[..., None]).astype(jnp.bfloat16)
            return current + jnp.einsum(
                "qhk,khd->qhd", weights, split_heads(block[1]), preferred_element_type=jnp.float32
            )

        return (lax.cond(jnp.min(block[2]) <= top_seg, out_compute, pass_state, inner), None)

    mixed = lax.scan(
        out_one_block,
        empty_heads,
        in_blocks(
            (
                lax.all_gather(keys, "ctx", axis=0, tiled=True),
                lax.all_gather(values, "ctx", axis=0, tiled=True),
                lax.all_gather(query_segs, "ctx", axis=0, tiled=True),
            )
        ),
    )[0]
    mixed_low = mixed.reshape(rows, -1).astype(jnp.bfloat16)
    self_branch = head_total(matmul(mixed_low, w_out)) + b_out[0]
    first, first_norm, first_inv = norm_forward(resid_in + self_branch, gains[0], shifts[0])
    first_low = first.astype(jnp.bfloat16)
    states_all = lax.all_gather(source_states, "ctx", axis=1, tiled=True)[0]
    cross_query = (matmul(first_low, w_cq) + b_attn[2]).astype(jnp.bfloat16)
    cross_keys = matmul(states_all, w_ckv[0]).astype(jnp.bfloat16)
    cross_values = (matmul(states_all, w_ckv[1]) + b_attn[3]).astype(jnp.bfloat16)
    cq_heads = split_heads(cross_query)
    ck_heads = split_heads(cross_keys)
    cv_heads = split_heads(cross_values)
    reach = jnp.arange(states_all.shape[0]) < source_len[0]
    cross_scores = jnp.einsum(
        "qhd,khd->qhk", cq_heads, ck_heads, preferred_element_type=jnp.float32
    ) * HEAD ** (-0.5)
    cross_scores = jnp.where(reach[None, None, :], cross_scores, NEG)
    cross_top = jnp.max(cross_scores, axis=-1, keepdims=True)
    powers = jnp.exp(cross_scores - cross_top)
    cross_weights = powers / jnp.sum(powers, axis=-1, keepdims=True)
    cross_low = cross_weights.astype(jnp.bfloat16)
    looked = (
        jnp.einsum("qhk,khd->qhd", cross_low, cv_heads, preferred_element_type=jnp.float32)
        .reshape(rows, -1)
        .astype(jnp.bfloat16)
    )
    cross_branch = head_total(matmul(looked, w_co)) + b_out[1]
    second, second_norm, second_inv = norm_forward(first + cross_branch, gains[1], shifts[1])
    second_low = second.astype(jnp.bfloat16)
    hidden = matmul(second_low, w_in) + ffn_in_bias
    sigma = 1.0 / (1.0 + jnp.exp(-hidden))
    active = (hidden / (1.0 + jnp.exp(-hidden))).astype(jnp.bfloat16)
    ffn_branch = head_total(matmul(active, w_fout)) + b_out[2]
    result, third_norm, third_inv = norm_forward(second + ffn_branch, gains[2], shifts[2])
    grad_third, gain_third, shift_third = norm_backward(
        out_grad[0].astype(jnp.float32), third_norm, third_inv, gains[2]
    )
    grad_ffn_low = grad_third.astype(jnp.bfloat16)
    grad_active = matmul_nt(grad_ffn_low, w_fout)
    grad_hidden = (grad_active * sigma * (1.0 + hidden * (1.0 - sigma))).astype(jnp.bfloat16)
    grad_second_in = grad_third + head_total(matmul_nt(grad_hidden, w_in))
    g_fin = matmul_tn(second_low, grad_hidden)
    g_fbias = jnp.sum(grad_hidden.astype(jnp.float32), axis=0)
    g_fout = matmul_tn(active, grad_ffn_low)
    grad_second, gain_second, shift_second = norm_backward(
        grad_second_in, second_norm, second_inv, gains[1]
    )
    grad_cross_low = grad_second.astype(jnp.bfloat16)
    grad_looked = matmul_nt(grad_cross_low, w_co).astype(jnp.bfloat16)
    gl_heads = split_heads(grad_looked)
    grad_cweights = jnp.einsum(
        "qhd,khd->qhk", gl_heads, cv_heads, preferred_element_type=jnp.float32
    )
    grad_cscores = cross_weights * (
        grad_cweights - jnp.sum(cross_weights * grad_cweights, axis=-1, keepdims=True)
    )
    grad_cscores = grad_cscores.astype(jnp.bfloat16)
    grad_cq = (
        (
            jnp.einsum("qhk,khd->qhd", grad_cscores, ck_heads, preferred_element_type=jnp.float32)
            * HEAD ** (-0.5)
        )
        .reshape(rows, -1)
        .astype(jnp.bfloat16)
    )
    part_ck = (
        jnp.einsum("qhk,qhd->khd", grad_cscores, cq_heads, preferred_element_type=jnp.float32)
        * HEAD ** (-0.5)
    ).reshape(states_all.shape[0], -1)
    part_cv = jnp.einsum(
        "qhk,qhd->khd", cross_low, gl_heads, preferred_element_type=jnp.float32
    ).reshape(states_all.shape[0], -1)
    grad_ck, grad_cv = in_one_piece(
        (part_ck.astype(jnp.bfloat16), part_cv.astype(jnp.bfloat16)), "ctx", 0, 1
    )
    grad_ck_low = grad_ck.astype(jnp.bfloat16)
    grad_cv_low = grad_cv.astype(jnp.bfloat16)
    local_states = source_states[0]
    g_ckv = jnp.stack([matmul_tn(local_states, grad_ck_low), matmul_tn(local_states, grad_cv_low)])
    source_part = matmul_nt(grad_ck_low, w_ckv[0]) + matmul_nt(grad_cv_low, w_ckv[1])
    grad_first_in = grad_second + head_total(matmul_nt(grad_cq, w_cq))
    g_cq = matmul_tn(first_low, grad_cq)
    g_co = matmul_tn(looked, grad_cross_low)
    grad_first, gain_first, shift_first = norm_backward(
        grad_first_in, first_norm, first_inv, gains[0]
    )
    grad_self_low = grad_first.astype(jnp.bfloat16)
    grad_mixed = matmul_nt(grad_self_low, w_out).astype(jnp.bfloat16)
    gm_heads = split_heads(grad_mixed)
    delta = jnp.sum(gm_heads.astype(jnp.float32) * mixed, axis=-1)

    def query_one_block(inner, block):

        def query_compute(current):
            block_keys = split_heads(block[0])
            scores = scores_of(query_heads, block_keys, query_segs, block[2])
            probs = jnp.exp(scores - log_sum[..., None])
            grad_probs = jnp.einsum(
                "qhd,khd->qhk", gm_heads, split_heads(block[1]), preferred_element_type=jnp.float32
            )
            grad_scores = (probs * (grad_probs - delta[..., None])).astype(jnp.bfloat16)
            return current + jnp.einsum(
                "qhk,khd->qhd", grad_scores, block_keys, preferred_element_type=jnp.float32
            )

        return (lax.cond(jnp.min(block[2]) <= top_seg, query_compute, pass_state, inner), None)

    grad_q_sum = lax.scan(
        query_one_block,
        empty_heads,
        in_blocks(
            (
                lax.all_gather(keys, "ctx", axis=0, tiled=True),
                lax.all_gather(values, "ctx", axis=0, tiled=True),
                lax.all_gather(query_segs, "ctx", axis=0, tiled=True),
            )
        ),
    )[0]
    all_log_sum, all_delta = (
        lax.all_gather(log_sum, "ctx", axis=0, tiled=True),
        lax.all_gather(delta, "ctx", axis=0, tiled=True),
    )

    def key_one_block(inner, block):
        remote_q, remote_grad, remote_segs, block_sum, block_delta = block

        def key_compute(current):
            grad_key_sum, grad_value_sum = current
            remote_heads = split_heads(remote_q)
            remote_grads = split_heads(remote_grad)
            scores = scores_of(remote_heads, key_heads, remote_segs, query_segs)
            probs = jnp.exp(scores - block_sum[..., None])
            grad_value_sum = grad_value_sum + jnp.einsum(
                "qhk,qhd->khd",
                probs.astype(jnp.bfloat16),
                remote_grads,
                preferred_element_type=jnp.float32,
            )
            grad_probs = jnp.einsum(
                "qhd,khd->qhk", remote_grads, value_heads, preferred_element_type=jnp.float32
            )
            grad_scores = (probs * (grad_probs - block_delta[..., None])).astype(jnp.bfloat16)
            grad_key_sum = grad_key_sum + jnp.einsum(
                "qhk,qhd->khd", grad_scores, remote_heads, preferred_element_type=jnp.float32
            )
            return (grad_key_sum, grad_value_sum)

        return (lax.cond(jnp.max(remote_segs) >= low_seg, key_compute, pass_state, inner), None)

    grad_k_sum, grad_v_sum = lax.scan(
        key_one_block,
        (empty_heads, empty_heads),
        in_blocks(
            (
                lax.all_gather(queries, "ctx", axis=0, tiled=True),
                lax.all_gather(grad_mixed, "ctx", axis=0, tiled=True),
                lax.all_gather(query_segs, "ctx", axis=0, tiled=True),
            )
            + (all_log_sum, all_delta)
        ),
    )[0]
    grad_q = (grad_q_sum * HEAD ** (-0.5)).reshape(rows, -1).astype(jnp.bfloat16)
    grad_k = (grad_k_sum * HEAD ** (-0.5)).reshape(rows, -1).astype(jnp.bfloat16)
    grad_v = grad_v_sum.reshape(rows, -1).astype(jnp.bfloat16)
    input_part = (
        matmul_nt(grad_q, w_qkv[0]) + matmul_nt(grad_k, w_qkv[1]) + matmul_nt(grad_v, w_qkv[2])
    )
    input_sum, source_sum = (
        lax.psum(input_part.astype(jnp.bfloat16), "tp").astype(jnp.float32),
        lax.psum(source_part.astype(jnp.bfloat16), "tp").astype(jnp.float32),
    )
    input_grad = grad_first + input_sum
    g_qkv = jnp.stack(
        [matmul_tn(inputs, grad_q), matmul_tn(inputs, grad_k), matmul_tn(inputs, grad_v)]
    )
    g_out = matmul_tn(mixed_low, grad_self_low)
    g_abias = jnp.stack(
        [
            jnp.sum(grad_q.astype(jnp.float32), axis=0),
            jnp.sum(grad_v.astype(jnp.float32), axis=0),
            jnp.sum(grad_cq.astype(jnp.float32), axis=0),
            jnp.sum(grad_cv_low.astype(jnp.float32), axis=0),
        ]
    )
    g_obias = jnp.stack(
        [jnp.sum(grad_first, axis=0), jnp.sum(grad_second, axis=0), jnp.sum(grad_third, axis=0)]
    )
    g_gain = jnp.stack([gain_first, gain_second, gain_third])
    g_shift = jnp.stack([shift_first, shift_second, shift_third])
    s_qkv, s_out, s_cq, s_ckv, s_co, s_fin, s_fout, s_abias, s_obias, s_gain, s_shift = lax.psum(
        (g_qkv, g_out, g_cq, g_ckv, g_co, g_fin, g_fout, g_abias, g_obias, g_gain, g_shift), "ctx"
    )
    o_qkv, o_out, o_cq, o_ckv, o_co, o_fin, o_fout, o_abias, o_obias, o_gain, o_shift = (
        lax.psum_scatter(
            s_qkv.astype(jnp.bfloat16), "fsdp", scatter_dimension=1, tiled=True
        ).astype(jnp.float32),
        lax.psum_scatter(
            s_out.astype(jnp.bfloat16), "fsdp", scatter_dimension=1, tiled=True
        ).astype(jnp.float32),
        lax.psum_scatter(s_cq.astype(jnp.bfloat16), "fsdp", scatter_dimension=0, tiled=True).astype(
            jnp.float32
        ),
        lax.psum_scatter(
            s_ckv.astype(jnp.bfloat16), "fsdp", scatter_dimension=1, tiled=True
        ).astype(jnp.float32),
        lax.psum_scatter(s_co.astype(jnp.bfloat16), "fsdp", scatter_dimension=1, tiled=True).astype(
            jnp.float32
        ),
        lax.psum_scatter(
            s_fin.astype(jnp.bfloat16), "fsdp", scatter_dimension=0, tiled=True
        ).astype(jnp.float32),
        lax.psum_scatter(
            s_fout.astype(jnp.bfloat16), "fsdp", scatter_dimension=1, tiled=True
        ).astype(jnp.float32),
        lax.psum_scatter(
            s_abias.astype(jnp.bfloat16), "fsdp", scatter_dimension=0, tiled=True
        ).astype(jnp.float32),
        lax.psum_scatter(
            s_obias.astype(jnp.bfloat16), "fsdp", scatter_dimension=1, tiled=True
        ).astype(jnp.float32),
        lax.psum_scatter(
            s_gain.astype(jnp.bfloat16), "fsdp", scatter_dimension=1, tiled=True
        ).astype(jnp.float32),
        lax.psum_scatter(
            s_shift.astype(jnp.bfloat16), "fsdp", scatter_dimension=1, tiled=True
        ).astype(jnp.float32),
    )
    squares = jnp.stack(
        [
            jnp.sum(resid_in * resid_in),
            jnp.sum(self_branch * self_branch),
            jnp.sum(cross_branch * cross_branch),
            jnp.sum(ffn_branch * ffn_branch),
        ]
    )
    fbias_total, square_total = lax.psum((g_fbias, squares), ("fsdp", "ctx"))
    entries = rows * inputs.shape[1] * lax.axis_size("fsdp") * lax.axis_size("ctx")
    rms_values = jnp.sqrt(square_total / entries)
    return (
        result[None].astype(jnp.bfloat16),
        input_grad[None],
        source_sum[None],
        rms_values,
        o_qkv,
        o_out,
        o_cq,
        o_ckv,
        o_co,
        o_fin,
        o_fout,
        o_abias,
        fbias_total,
        o_obias,
        o_gain,
        o_shift,
    )


def solution(mesh):
    in_specs = (
        P("fsdp", "ctx", None),
        P("fsdp", "ctx", None),
        P("fsdp", "ctx"),
        P("fsdp"),
        P("fsdp", "ctx", None),
        P(None, "fsdp", "tp"),
        P("tp", "fsdp"),
        P("fsdp", "tp"),
        P(None, "fsdp", "tp"),
        P("tp", "fsdp"),
        P("fsdp", "tp"),
        P("tp", "fsdp"),
        P("fsdp", "tp"),
        P("tp"),
        P(None, "fsdp"),
        P(None, "fsdp"),
        P(None, "fsdp"),
    )
    out_specs = (
        P("fsdp", "ctx", None),
        P("fsdp", "ctx", None),
        P("fsdp", "ctx", None),
        P(),
        P(None, "fsdp", "tp"),
        P("tp", "fsdp"),
        P("fsdp", "tp"),
        P(None, "fsdp", "tp"),
        P("tp", "fsdp"),
        P("fsdp", "tp"),
        P("tp", "fsdp"),
        P("fsdp", "tp"),
        P("tp"),
        P(None, "fsdp"),
        P(None, "fsdp"),
        P(None, "fsdp"),
    )
    return jax.shard_map(
        per_device, mesh=mesh, in_specs=in_specs, out_specs=out_specs, check_vma=False
    )
```

profile of v0, /device:TPU:0, one launch (start us, length us, event | category | flops | bytes accessed | tf_op | source)
XLA Modules:
  0.0 900.3 jit_solution(10636245896675517203)
XLA Ops:
  19.0 22.2 %all-gather = s32[1,2048]{1,0:T(1,128)S(1)} all-gather(s32[1,256]{1,0:T(1,128)S(1)} %copy-done.31), channel_id=2, replica_groups=mesh['fsdp'=2,'ctx'=8,'tp'=2] {'ctx'}, dimensions={1}, use_global_device_ids=true | all-gather | bytes 9216 | tf_op jit(solution)/shard_map/all_gather | solution.py:190
  62.0 33.7 %all-gather.12.cloned.1.call-done = bf16[2048,256]{0,1:T(8,128)(2,1)} async-done(((bf16[256,256]{0,1:T(8,128)(2,1)}), bf16[2048,256]{0,1:T(8,128)(2,1)}) %all-gather.12.cloned.1.call-update) | async-done | bytes 1048592 | tf_op jit(solution)/shard_map/all_gather | solution.py:189
  98.0 11.6 %while.50 = (s32[]{:T(128)}, f32[256,4]{0,1:T(4,128)S(1)}, f32[256,4]{0,1:T(4,128)S(1)}, s32[4,512]{1,0:T(4,128)}, s32[]{:T(128)}, /*index=5*/s32[1,256]{1,0:T(1...) while((s32[]{:T(128)}, f32[256,4]{0,1:T(4,128)S(1)}, ...), condition=%wide.region_7.8_spmd, body=%wide.region_1.7_spmd.sunk | while | flops 70912512 | bytes 5565663 | solution.py:160
  109.7 12.4 %while.51 = (s32[]{:T(128)}, f32[256,4,64]{0,2,1:T(8,128)S(1)}, s32[4,512]{1,0:T(4,128)}, s32[]{:T(128)}, s32[1,256]{1,0:T(1,128)S(1)}, /*index=5*/bf16[4,512,25...) while((s32[]{:T(128)}, f32[256,4,64]{0,2,1:T(8,128)S(1)}, ...), condition=%wide.region_12.13_spmd, body=%wide.region_8.0_spmd.sunk | while | flops 136512000 | bytes 2501839 | solution.py:183
  123.2 14.0 %all-gather.14.cloned.1.call-done = bf16[1,1024,512]{2,1,0:T(8,128)(2,1)} async-done(((bf16[1,128,512]{2,1,0:T(8,128)(2,1)}), bf16[1,1024,512]{2,1,0:T(8,128)(2,1)}) %all-gather.14.cloned.1.call-update) | async-done | bytes 1048592 | tf_op jit(solution)/shard_map/all_gather | solution.py:198
  140.4 21.6 %all-reduce.12.cloned.1.call-done = bf16[256,512]{1,0:T(8,128)(2,1)} async-done(((bf16[256,512]{1,0:T(8,128)(2,1)}), bf16[256,512]{1,0:T(8,128)(2,1)}) %all-reduce.12.cloned.1.call-update) | async-done | bytes 262160 | tf_op jit(solution)/shard_map/psum | solution.py:129
  175.3 21.7 %all-reduce.14.cloned.1.call-done = bf16[256,512]{1,0:T(8,128)(2,1)} async-done(((bf16[256,512]{1,0:T(8,128)(2,1)}), bf16[256,512]{1,0:T(8,128)(2,1)}) %all-reduce.14.cloned.1.call-update) | async-done | bytes 262160 | tf_op jit(solution)/shard_map/psum | solution.py:129
  205.4 32.8 %all-gather.20.cloned.1.call-done = bf16[2048,256]{0,1:T(8,128)(2,1)} async-done(((bf16[256,256]{0,1:T(8,128)(2,1)}), bf16[2048,256]{0,1:T(8,128)(2,1)}) %all-gather.20.cloned.1.call-update) | async-done | bytes 1048592 | tf_op jit(solution)/shard_map/all_gather | solution.py:347
  240.6 31.9 %all_gather.79 = f32[2048,4]{0,1:T(4,128)} all-gather(f32[256,4]{0,1:T(4,128)S(1)} %copy-done.52), channel_id=1, replica_groups=mesh['fsdp'=2,'ctx'=8,'tp'=2] {'ctx'}, dimensions={0}, use_global_device_ids=true | all-gather | bytes 36864 | tf_op jit(solution)/shard_map/all_gather | solution.py:312
  284.0 19.1 %all-reduce.18.cloned.1.call-done = bf16[256,512]{1,0:T(8,128)(2,1)} async-done(((bf16[256,512]{1,0:T(8,128)(2,1)}), bf16[256,512]{1,0:T(8,128)(2,1)}) %all-reduce.18.cloned.1.call-update) | async-done | bytes 262160 | tf_op jit(solution)/shard_map/psum | solution.py:129
  317.7 5.5 all-to-all-start
  326.2 12.5 %all-reduce.20.cloned.1.call-done = bf16[256,512]{1,0:T(8,128)(2,1)} async-done(((bf16[256,512]{1,0:T(8,128)(2,1)}), bf16[256,512]{1,0:T(8,128)(2,1)}) %all-reduce.20.cloned.1.call-update) | async-done | bytes 262160 | tf_op jit(solution)/shard_map/psum | solution.py:129
  345.2 16.2 %while.52 = (s32[]{:T(128)}, f32[256,4,64]{0,2,1:T(8,128)}, s32[4,512]{1,0:T(4,128)}, s32[]{:T(128)}, s32[1,256]{1,0:T(1,128)S(1)}, /*index=5*/bf16[4,512,256]{1...) while((s32[]{:T(128)}, f32[256,4,64]{0,2,1:T(8,128)}, ...), condition=%wide.region_38.39_spmd, body=%wide.region_34.38_spmd.sunk | while | flops 204669440 | bytes 7093487 | solution.py:300
  347.7 5.9 conditional.10
  369.2 50.1 %all_gather.81 = f32[2048,4]{0,1:T(4,128)} all-gather(f32[256,4]{0,1:T(4,128)S(1)} %get-tuple-element.1401), channel_id=1, replica_groups=mesh['fsdp'=2,'ctx'=8,'tp'=2] {'ctx'}, dimensions={0}, use_global_device_ids=true | all-gather | bytes 36864 | tf_op jit(solution)/shard_map/all_gather | solution.py:313
  430.1 29.1 %while.53 = (s32[]{:T(128)}, f32[256,4,64]{0,2,1:T(8,128)S(1)}, f32[256,4,64]{0,2,1:T(8,128)S(1)}, s32[4,512]{1,0:T(4,128)}, s32[]{:T(128)}, /*index=5*/s32[1,25...) while((s32[]{:T(128)}, f32[256,4,64]{0,2,1:T(8,128)S(1)}, ...), condition=%wide.region_44.45_spmd, body=%wide.region_40.44_spmd.sunk | while | flops 272368128 | bytes 10018083 | solution.py:342
  440.0 4.6 conditional.11
  454.5 4.6 conditional.11
  461.7 319.1 %all-reduce.23 = (bf16[3,512,256]{1,2,0:T(8,128)(2,1)}, bf16[2,512,256]{1,2,0:T(8,128)(2,1)}, bf16[256,512]{1,0:T(8,128)(2,1)}, bf16[512,256]{1,0:T(8,128)(2,1)}...) all-reduce(f32[3,512,256]{1,2,0:T(8,128)} %pad_maximum_fusion, ...), channel_id=1, replica_groups=mesh['fsdp'=2,'ctx'=8,'tp'=2] {'ctx'}, use_global_device_ids=true, to_apply=%region_53.54 | all-reduce | flops 2102784 | bytes 12616704 | tf_op jit(solution)/shard_map/psum | solution.py:382
  796.1 33.3 %all-reduce.1 = (f32[4]{0:T(128)S(1)}, f32[1024]{0:T(1024)}) all-reduce(f32[4]{0:T(128)S(1)} %pad_maximum_fusion.7, f32[1024]{0:T(1024)S(1)} %copy-done.69), channel_id=1, replica_groups=mesh['fsdp'=2,'ctx'=8,'tp'=2] {'fsdp','ctx'}, use_global_device_ids=true, to_apply=%region_52.53 | all-reduce | flops 1028 | bytes 8224 | tf_op jit(solution)/shard_map/psum | solution.py:428
  845.9 9.4 %reduce-scatter.23.cloned.1.call-done = bf16[2,256,256]{1,2,0:T(8,128)(2,1)} async-done(((bf16[2,512,256]{1,2,0:T(8,128)(2,1)}), bf16[2,256,256]{1,2,0:T(8,128)(2,1)}) %reduce-scatter.23.cloned.1.call-update) | async-done | bytes 262160 | tf_op jit(solution)/shard_map/reduce_scatter | solution.py:395
  857.2 9.6 %reduce-scatter.17.cloned.1.call-done = bf16[3,256,256]{1,2,0:T(8,128)(2,1)} async-done(((bf16[3,512,256]{1,2,0:T(8,128)(2,1)}), bf16[3,256,256]{1,2,0:T(8,128)(2,1)}) %reduce-scatter.17.cloned.1.call-update) | async-done | bytes 393232 | tf_op jit(solution)/shard_map/reduce_scatter | solution.py:386
  868.9 10.1 %reduce-scatter.27.cloned.1.call-done = bf16[256,1024]{1,0:T(8,128)(2,1)} async-done(((bf16[512,1024]{1,0:T(8,128)(2,1)}), bf16[256,1024]{1,0:T(8,128)(2,1)}) %reduce-scatter.27.cloned.1.call-update) | async-done | bytes 524304 | tf_op jit(solution)/shard_map/reduce_scatter | solution.py:401
  881.1 9.7 %reduce-scatter.29.cloned.1.call-done = bf16[1024,256]{1,0:T(8,128)(2,1)} async-done(((bf16[1024,512]{1,0:T(8,128)(2,1)}), bf16[1024,256]{1,0:T(8,128)(2,1)}) %reduce-scatter.29.cloned.1.call-update) | async-done | bytes 524304 | tf_op jit(solution)/shard_map/reduce_scatter | solution.py:404
  (422 shorter events, 218.3 us)
Async XLA Ops:
  8.1 52.6 %all-gather.10.cloned.1.call-start = ((), (), s32[]{:S(2)}) async-start(), calls=%async_computation.11 | async-start | bytes 1179648 | tf_op jit(solution)/shard_map/all_gather | solution.py:188
  13.1 82.6 %all-gather.12.cloned.1.call-start = ((), (), s32[]{:S(2)}) async-start(), calls=%async_computation.12 | async-start | bytes 1179648 | tf_op jit(solution)/shard_map/all_gather | solution.py:189
  18.2 119.0 %all-gather.14.cloned.1.call-start = ((), (), s32[]{:S(2)}) async-start(), calls=%async_computation.14 | async-start | bytes 1179648 | tf_op jit(solution)/shard_map/all_gather | solution.py:198
  18.9 143.0 %all-reduce.12.cloned.1.call-start = ((), (), s32[]{:S(2)}) async-start(), calls=%async_computation.13 | async-start | bytes 524288 | tf_op jit(solution)/shard_map/psum | solution.py:129
  123.2 73.8 %all-reduce.14.cloned.1.call-start = ((), (), s32[]{:S(2)}) async-start(), calls=%async_computation.15 | async-start | bytes 524288 | tf_op jit(solution)/shard_map/psum | solution.py:129
  173.5 25.6 %all-gather.16.cloned.1.call-start = ((), (), s32[]{:S(2)}) async-start(), calls=%async_computation.16 | async-start | bytes 1572864 | tf_op jit(solution)/shard_map/all_gather | solution.py:112
  174.1 27.8 %all-gather.18.cloned.1.call-start = ((), (), s32[]{:S(2)}) async-start(), calls=%async_computation.17 | async-start | bytes 1572864 | tf_op jit(solution)/shard_map/all_gather | solution.py:113
  174.7 63.6 %all-gather.20.cloned.1.call-start = ((), (), s32[]{:S(2)}) async-start(), calls=%async_computation.21 | async-start | bytes 1179648 | tf_op jit(solution)/shard_map/all_gather | solution.py:347
  175.3 97.2 %all-reduce.16.cloned.1.call-start = ((), (), s32[]{:S(2)}) async-start(), calls=%async_computation.18 | async-start | bytes 524288 | tf_op jit(solution)/shard_map/psum | solution.py:129
  204.7 98.4 %all-reduce.18.cloned.1.call-start = ((), (), s32[]{:S(2)}) async-start(), calls=%async_computation.19 | async-start | bytes 524288 | tf_op jit(solution)/shard_map/psum | solution.py:129
  280.9 57.8 %all-reduce.20.cloned.1.call-start = ((), (), s32[]{:S(2)}) async-start(), calls=%async_computation.20 | async-start | bytes 524288 | tf_op jit(solution)/shard_map/psum | solution.py:129
  317.7 105.5 %all-to-all-start = ((bf16[8,128,512]{1,2,0:T(8,128)(2,1)}), bf16[8,128,512]{1,2,0:T(8,128)(2,1)}, u32[]{:S(2)}, u32[]{:S(2)}) async-start(bf16[8,128,512]{1,2,0:T(8,128)(2,1)} %pad_maximum_fusion.1), calls=%async_computation | async-start | bytes 2097152 | tf_op jit(solution)/shard_map/all_to_all | solution.py:20
  323.2 104.5 %all-gather.22.cloned.1.call-start = ((), (), s32[]{:S(2)}) async-start(), calls=%async_computation.22 | async-start | bytes 1179648 | tf_op jit(solution)/shard_map/all_gather | solution.py:348
  344.4 488.6 %reduce-scatter.31.cloned.1.call-start = ((), (), s32[]{:S(2)}) async-start(), calls=%async_computation.30 | async-start | bytes 196608
  781.6 52.9 %reduce-scatter.33.cloned.1.call-start = ((), (), s32[]{:S(2)}) async-start(), calls=%async_computation.31 | async-start | bytes 196608
  784.4 51.7 %reduce-scatter.35.cloned.1.call-start = ((), (), s32[]{:S(2)}) async-start(), calls=%async_computation.32 | async-start | bytes 196608
  786.6 51.0 %all-reduce.22.cloned.1.call-start = ((), (), s32[]{:S(2)}) async-start(), calls=%async_computation.33 | async-start | bytes 786432 | tf_op jit(solution)/shard_map/psum | solution.py:361
  787.6 53.4 %reduce-scatter.19.cloned.1.call-start = ((), (), s32[]{:S(2)}) async-start(), calls=%async_computation.24 | async-start | bytes 393216 | tf_op jit(solution)/shard_map/reduce_scatter | solution.py:389
  788.2 54.4 %reduce-scatter.21.cloned.1.call-start = ((), (), s32[]{:S(2)}) async-start(), calls=%async_computation.25 | async-start | bytes 393216 | tf_op jit(solution)/shard_map/reduce_scatter | solution.py:392
  788.8 55.5 %reduce-scatter.25.cloned.1.call-start = ((), (), s32[]{:S(2)}) async-start(), calls=%async_computation.27 | async-start | bytes 393216 | tf_op jit(solution)/shard_map/reduce_scatter | solution.py:398
  789.6 65.8 %reduce-scatter.23.cloned.1.call-start = ((), (), s32[]{:S(2)}) async-start(), calls=%async_computation.26 | async-start | bytes 786432 | tf_op jit(solution)/shard_map/reduce_scatter | solution.py:395
  790.2 76.7 %reduce-scatter.17.cloned.1.call-start = ((), (), s32[]{:S(2)}) async-start(), calls=%async_computation.23 | async-start | bytes 1179648 | tf_op jit(solution)/shard_map/reduce_scatter | solution.py:386
  790.9 88.1 %reduce-scatter.27.cloned.1.call-start = ((), (), s32[]{:S(2)}) async-start(), calls=%async_computation.28 | async-start | bytes 1572864 | tf_op jit(solution)/shard_map/reduce_scatter | solution.py:401
  791.5 99.3 %reduce-scatter.29.cloned.1.call-start = ((), (), s32[]{:S(2)}) async-start(), calls=%async_computation.29 | async-start | bytes 1572864 | tf_op jit(solution)/shard_map/reduce_scatter | solution.py:404
  (79 other events, 2398.6 us)
Sparse Core Ops, SparseCore 0:
  13.2 41.9 all-gather.9
  57.3 38.3 all-gather.11
  97.9 39.2 all-gather.13
  139.9 21.9 all-reduce.11
  173.6 23.2 all-reduce.13
  204.8 23.2 all-reduce.15
  281.0 22.0 all-reduce.17
  315.4 23.2 all-reduce.19
  790.9 24.6 all-reduce.21
Sparse Core Ops, SparseCore 1:
  175.5 8.9 all-gather.15
  185.9 9.8 all-gather.17
  197.7 40.5 all-gather.19
  344.5 39.2 all-gather.21
  781.7 6.3 reduce-scatter.30
  790.8 8.6 reduce-scatter.32
  802.1 8.6 reduce-scatter.34
  813.5 8.8 reduce-scatter.18
  824.4 8.8 reduce-scatter.20
  835.4 8.8 reduce-scatter.24
  846.4 8.9 reduce-scatter.22
  857.6 9.2 reduce-scatter.16
  869.5 9.4 reduce-scatter.26
  881.3 9.5 reduce-scatter.28
where the time goes:
time: 904 us; the launch traced here: 900 us
  blocking collectives  477 us (53%)
  waiting for transfers between devices  201 us (22%)
  other arithmetic  71.5 us (8%)
  matrix products  67.8 us (8%)
  local copies, waits for them, and re-layouts  37.9 us (4%)
  loops' own time  20.3 us (2%)
  between operations  18.1 us (2%)
    psum x1, blocking collectives, per_device(): lax.psum((g_qkv, g_out, g_cq, g_ckv, g_co, g_fin, g_fout, g_abias, g_obia...  319 us
    psum x5, waiting for transfers between devices, head_total(): lax.psum(partial_value.astype(jnp.bfloat16), 'tp').astype(jnp.float32)  74.8 us
    all_gather x1, blocking collectives, per_device(): lax.all_gather(delta, 'ctx', axis=0, tiled=True)  50.1 us
    all_gather x1, waiting for transfers between devices, per_device(): lax.all_gather(values, 'ctx', axis=0, tiled=True)  33.7 us
    psum x1, blocking collectives, per_device(): fbias_total, square_total = lax.psum((g_fbias, squares), ('fsdp', 'ctx'))  33.3 us
    all_gather x1, waiting for transfers between devices, per_device(): lax.all_gather(queries, 'ctx', axis=0, tiled=True)  32.8 us
    all_gather x1, blocking collectives, per_device(): lax.all_gather(log_sum, 'ctx', axis=0, tiled=True)  31.9 us
    all_gather x1, blocking collectives, per_device(): lax.all_gather(query_segs, 'ctx', axis=0, tiled=True)  22.2 us
  transfers between devices with their start and end apart: 24, of which 11 were waited for; matrix products, arithmetic and copies ran while one was open for 12% of the time, Pallas kernels for 0%

commit v1 on v0

--- a/solution.py
+++ b/solution.py
@@ -28,6 +28,38 @@
         done.append(lax.slice_in_dim(out, at, at + a.shape[along], axis=along))
         at += a.shape[along]
     return tuple(done)
+
+
+def other(axis):
+    size = lax.axis_size(axis)
+    return [(i, (i + size // 2) % size) for i in range(size)]
+
+
+def tp_total(part):
+    return part.astype(jnp.float32) + lax.ppermute(part, "tp", other("tp")).astype(jnp.float32)
+
+
+def pair_scatter(x, dim):
+    half = x.shape[dim] // 2
+    me = lax.axis_index("fsdp")
+    sent = lax.dynamic_slice_in_dim(x, (1 - me) * half, half, dim).astype(jnp.bfloat16)
+    kept = lax.dynamic_slice_in_dim(x, me * half, half, dim)
+    return kept + lax.ppermute(sent, "fsdp", other("fsdp")).astype(jnp.float32)
+
+
+def gather_by_exchange(x, axis):
+    size = lax.axis_size(axis)
+    return lax.all_to_all(
+        jnp.broadcast_to(x[None], (size,) + x.shape), axis, split_axis=0, concat_axis=0, tiled=True
+    )
+
+
+def ctx_total(x):
+    size = lax.axis_size("ctx")
+    pieces = x.reshape(size, -1, x.shape[1])
+    arrived = lax.all_to_all(pieces, "ctx", split_axis=0, concat_axis=0, tiled=True)
+    mine = arrived.astype(jnp.float32).sum(axis=0).astype(jnp.bfloat16)
+    return gather_by_exchange(mine, "ctx").reshape(x.shape)
 
 
 def matmul(left, right):
@@ -126,7 +158,7 @@
     )
 
     def head_total(partial_value):
-        return lax.psum(partial_value.astype(jnp.bfloat16), "tp").astype(jnp.float32)
+        return tp_total(partial_value.astype(jnp.bfloat16))
 
     inputs = tokens[0]
     resid_in = inputs.astype(jnp.float32)
@@ -144,6 +176,14 @@
     start_state = (jnp.full((rows, heads), NEG, jnp.float32), jnp.zeros((rows, heads), jnp.float32))
     empty_heads = jnp.zeros((rows, heads, HEAD), jnp.float32)
 
+    def over_ctx(x):
+        stacked = gather_by_exchange(x, "ctx")
+        return stacked.reshape((-1,) + x.shape[1:])
+
+    both = over_ctx(jnp.concatenate([keys, values], axis=1))
+    all_keys, all_values = both[:, : keys.shape[1]], both[:, keys.shape[1] :]
+    all_segs = over_ctx(query_segs)
+
     def stat_one_block(inner, block):
 
         def stat_compute(current):
@@ -162,8 +202,8 @@
         start_state,
         in_blocks(
             (
-                lax.all_gather(keys, "ctx", axis=0, tiled=True),
-                lax.all_gather(query_segs, "ctx", axis=0, tiled=True),
+                all_keys,
+                all_segs,
             )
         ),
     )[0]
@@ -185,9 +225,9 @@
         empty_heads,
         in_blocks(
             (
-                lax.all_gather(keys, "ctx", axis=0, tiled=True),
-                lax.all_gather(values, "ctx", axis=0, tiled=True),
-                lax.all_gather(query_segs, "ctx", axis=0, tiled=True),
+                all_keys,
+                all_values,
+                all_segs,
             )
         ),
     )[0]
@@ -195,7 +235,7 @@
     self_branch = head_total(matmul(mixed_low, w_out)) + b_out[0]
     first, first_norm, first_inv = norm_forward(resid_in + self_branch, gains[0], shifts[0])
     first_low = first.astype(jnp.bfloat16)
-    states_all = lax.all_gather(source_states, "ctx", axis=1, tiled=True)[0]
+    states_all = over_ctx(source_states[0])
     cross_query = (matmul(first_low, w_cq) + b_attn[2]).astype(jnp.bfloat16)
     cross_keys = matmul(states_all, w_ckv[0]).astype(jnp.bfloat16)
     cross_values = (matmul(states_all, w_ckv[1]) + b_attn[3]).astype(jnp.bfloat16)
@@ -302,15 +342,15 @@
         empty_heads,
         in_blocks(
             (
-                lax.all_gather(keys, "ctx", axis=0, tiled=True),
-                lax.all_gather(values, "ctx", axis=0, tiled=True),
-                lax.all_gather(query_segs, "ctx", axis=0, tiled=True),
+                all_keys,
+                all_values,
+                all_segs,
             )
         ),
     )[0]
     all_log_sum, all_delta = (
-        lax.all_gather(log_sum, "ctx", axis=0, tiled=True),
-        lax.all_gather(delta, "ctx", axis=0, tiled=True),
+        over_ctx(log_sum),
+        over_ctx(delta),
     )
 
     def key_one_block(inner, block):
@@ -344,9 +384,9 @@
         (empty_heads, empty_heads),
         in_blocks(
             (
-                lax.all_gather(queries, "ctx", axis=0, tiled=True),
-                lax.all_gather(grad_mixed, "ctx", axis=0, tiled=True),
-                lax.all_gather(query_segs, "ctx", axis=0, tiled=True),
+                over_ctx(queries),
+                over_ctx(grad_mixed),
+                all_segs,
             )
             + (all_log_sum, all_delta)
         ),
@@ -358,8 +398,8 @@
         matmul_nt(grad_q, w_qkv[0]) + matmul_nt(grad_k, w_qkv[1]) + matmul_nt(grad_v, w_qkv[2])
     )
     input_sum, source_sum = (
-        lax.psum(input_part.astype(jnp.bfloat16), "tp").astype(jnp.float32),
-        lax.psum(source_part.astype(jnp.bfloat16), "tp").astype(jnp.float32),
+        tp_total(input_part.astype(jnp.bfloat16)),
+        tp_total(source_part.astype(jnp.bfloat16)),
     )
     input_grad = grad_first + input_sum
     g_qkv = jnp.stack(
@@ -379,44 +419,31 @@
     )
     g_gain = jnp.stack([gain_first, gain_second, gain_third])
     g_shift = jnp.stack([shift_first, shift_second, shift_third])
-    s_qkv, s_out, s_cq, s_ckv, s_co, s_fin, s_fout, s_abias, s_obias, s_gain, s_shift = lax.psum(
-        (g_qkv, g_out, g_cq, g_ckv, g_co, g_fin, g_fout, g_abias, g_obias, g_gain, g_shift), "ctx"
-    )
-    o_qkv, o_out, o_cq, o_ckv, o_co, o_fin, o_fout, o_abias, o_obias, o_gain, o_shift = (
-        lax.psum_scatter(
-            s_qkv.astype(jnp.bfloat16), "fsdp", scatter_dimension=1, tiled=True
-        ).astype(jnp.float32),
-        lax.psum_scatter(
-            s_out.astype(jnp.bfloat16), "fsdp", scatter_dimension=1, tiled=True
-        ).astype(jnp.float32),
-        lax.psum_scatter(s_cq.astype(jnp.bfloat16), "fsdp", scatter_dimension=0, tiled=True).astype(
-            jnp.float32
-        ),
-        lax.psum_scatter(
-            s_ckv.astype(jnp.bfloat16), "fsdp", scatter_dimension=1, tiled=True
-        ).astype(jnp.float32),
-        lax.psum_scatter(s_co.astype(jnp.bfloat16), "fsdp", scatter_dimension=1, tiled=True).astype(
-            jnp.float32
-        ),
-        lax.psum_scatter(
-            s_fin.astype(jnp.bfloat16), "fsdp", scatter_dimension=0, tiled=True
-        ).astype(jnp.float32),
-        lax.psum_scatter(
-            s_fout.astype(jnp.bfloat16), "fsdp", scatter_dimension=1, tiled=True
-        ).astype(jnp.float32),
-        lax.psum_scatter(
-            s_abias.astype(jnp.bfloat16), "fsdp", scatter_dimension=0, tiled=True
-        ).astype(jnp.float32),
-        lax.psum_scatter(
-            s_obias.astype(jnp.bfloat16), "fsdp", scatter_dimension=1, tiled=True
-        ).astype(jnp.float32),
-        lax.psum_scatter(
-            s_gain.astype(jnp.bfloat16), "fsdp", scatter_dimension=1, tiled=True
-        ).astype(jnp.float32),
-        lax.psum_scatter(
-            s_shift.astype(jnp.bfloat16), "fsdp", scatter_dimension=1, tiled=True
-        ).astype(jnp.float32),
-    )
+    big = (
+        (g_qkv, 1),
+        (g_out, 1),
+        (g_cq, 0),
+        (g_ckv, 1),
+        (g_co, 1),
+        (g_fin, 0),
+        (g_fout, 1),
+        (g_abias, 0),
+        (g_obias, 1),
+        (g_gain, 1),
+        (g_shift, 1),
+    )
+    halves = [pair_scatter(g, dim) for g, dim in big]
+    flats = [h.astype(jnp.bfloat16).reshape(-1) for h in halves]
+    size = lax.axis_size("ctx")
+    lengths = [f.shape[0] for f in flats]
+    pad = -sum(lengths) % (512 * 16 * size)
+    packed = jnp.concatenate(flats + [jnp.zeros((pad,), jnp.bfloat16)]).reshape(-1, 512)
+    summed = ctx_total(packed).reshape(-1).astype(jnp.float32)
+    outs, at = [], 0
+    for h, length in zip(halves, lengths):
+        outs.append(summed[at : at + length].reshape(h.shape))
+        at += length
+    o_qkv, o_out, o_cq, o_ckv, o_co, o_fin, o_fout, o_abias, o_obias, o_gain, o_shift = outs
     squares = jnp.stack(
         [
             jnp.sum(resid_in * resid_in),

time: 904 us -> 565 us (0.62)
  blocking collectives: 477 us -> 164 us
  waiting for transfers between devices: 201 us -> 90.9 us
  starting transfers between devices: 6.47 us -> 76.2 us
  local copies, waits for them, and re-layouts: 37.9 us -> 79 us
  matrix products: 67.8 us -> 52.4 us
  other arithmetic: 71.5 us -> 62.2 us
    psum x1 -> x0, blocking collectives: 319 us -> none  [per_device(): lax.psum((g_qkv, g_out, g_cq, g_ckv, g_co, g_fin, g_fout, g_abias, g_obia...]
    all_gather x3 -> x0, blocking collectives: 104 us -> none  [the longest x1 50.1 us: per_device(): lax.all_gather(delta, 'ctx', axis=0, tiled=True)]
    all_gather x5 -> x0, waiting for transfers between devices: 80.6 us -> none  [the longest x1 33.7 us: per_device(): lax.all_gather(values, 'ctx', axis=0, tiled=True)]
    psum x6 -> x0, waiting for transfers between devices: 74.8 us -> none  [the longest x5 74.8 us: head_total(): lax.psum(partial_value.astype(jnp.bfloat16), 'tp').astype(jnp.float32)]
    all_to_all x0 -> x2, blocking collectives: none -> 69.3 us  [the longest x1 55.7 us: ctx_total(): lax.all_to_all(pieces, 'ctx', split_axis=0, concat_axis=0, tiled=True)]
    all_to_all x0 -> x7, waiting for transfers between devices: none -> 66 us  [gather_by_exchange(): lax.all_to_all(jnp.broadcast_to(x[None], (size,) + x.shape), axis, split_...]
    all_to_all x0 -> x7, starting transfers between devices: none -> 60.4 us  [gather_by_exchange(): lax.all_to_all(jnp.broadcast_to(x[None], (size,) + x.shape), axis, split_...]
    reduce_scatter x7 -> x0, waiting for transfers between devices: 38.9 us -> none  [the longest x1 10.1 us: per_device(): lax.psum_scatter(s_fin.astype(jnp.bfloat16), 'fsdp', scatter_dimension=0,...]
  transfers between devices with their start and end apart: 24 -> 28, of which waited for: 11 -> 11; matrix products, arithmetic and copies ran while one was open for 12% -> 27% of each run, Pallas kernels for 0% -> 0%
where the time goes in v1:
time: 565 us; the launch traced here: 562 us
  blocking collectives  164 us (29%)
  waiting for transfers between devices  90.9 us (16%)
  local copies, waits for them, and re-layouts  79 us (14%)
  starting transfers between devices  76.2 us (13%)
  other arithmetic  62.2 us (11%)
  matrix products  52.4 us (9%)
  loops' own time  20.6 us (4%)
  between operations  16.2 us (3%)
    psum x1, blocking collectives, per_device(): fbias_total, square_total = lax.psum((g_fbias, squares), ('fsdp', 'ctx'))  71.9 us
    all_to_all x7, waiting for transfers between devices, gather_by_exchange(): lax.all_to_all(jnp.broadcast_to(x[None], (size,) + x.shape), axis, split_...  66 us
    all_to_all x7, starting transfers between devices, gather_by_exchange(): lax.all_to_all(jnp.broadcast_to(x[None], (size,) + x.shape), axis, split_...  60.4 us
    all_to_all x1, blocking collectives, ctx_total(): lax.all_to_all(pieces, 'ctx', split_axis=0, concat_axis=0, tiled=True)  55.7 us
    ppermute x7, waiting for transfers between devices, tp_total(): lax.ppermute(part, 'tp', other('tp')).astype(jnp.float32)  14.2 us
    all_to_all x1, blocking collectives, gather_by_exchange(): lax.all_to_all(jnp.broadcast_to(x[None], (size,) + x.shape), axis, split_...  13.6 us
    unnamed x207, local copies, waits for them, and re-layouts  13.1 us
    dot_general x10, matrix products, matmul(): return jnp.dot(left, right, preferred_element_type=jnp.float32)  12.7 us
  transfers between devices with their start and end apart: 28, of which 11 were waited for; matrix products, arithmetic and copies ran while one was open for 27% of the time, Pallas kernels for 0%

profile of v1, /device:TPU:0, one launch (start us, length us, event | category | flops | bytes accessed | tf_op | source)
XLA Modules:
  0.0 561.8 jit_solution(7630005832586333705)
XLA Ops:
  7.9 13.6 %all_to_all.51 = s32[8,1,256]{2,1,0:T(1,128)S(1)} all-to-all(s32[8,1,256]{2,1,0:T(1,128)S(1)} %broadcast_in_dim.164), channel_id=1, replica_groups=mesh['fsdp'=2,'ctx'=8,'tp'=2] {'ctx'}, dimensions={0} | all-to-all | bytes 16384 | tf_op jit(solution)/shard_map/all_to_all | solution.py:52
  33.1 18.8 %all-to-all-done.2 = bf16[8,128,512]{2,1,0:T(8,128)(2,1)S(1)} async-done(((bf16[8,128,512]{2,1,0:T(8,128)(2,1)}), bf16[8,128,512]{2,1,0:T(8,128)(2,1)S(1)}, u32[]{:S(2)}, u32[]{:S(2)}) %all-to-all-start.2) | async-done | bytes 1048608 | tf_op jit(solution)/shard_map/all_to_all | solution.py:52
  86.0 19.5 %all-to-all-done.1 = bf16[8,256,512]{2,1,0:T(8,128)(2,1)S(1)} async-done(((bf16[8,256,512]{2,1,0:T(8,128)(2,1)}), bf16[8,256,512]{2,1,0:T(8,128)(2,1)S(1)}, u32[]{:S(2)}, u32[]{:S(2)}) %all-to-all-start.1) | async-done | bytes 2097184 | tf_op jit(solution)/shard_map/all_to_all | solution.py:52
  108.5 11.7 %while.50 = (s32[]{:T(128)}, f32[256,4]{0,1:T(4,128)S(1)}, f32[256,4]{0,1:T(4,128)S(1)}, s32[4,512]{1,0:T(4,128)}, s32[]{:T(128)}, /*index=5*/s32[1,256]{1,0:T(1...) while((s32[]{:T(128)}, f32[256,4]{0,1:T(4,128)S(1)}, ...), condition=%wide.region_7.8_spmd, body=%wide.region_1.7_spmd.sunk | while | flops 70912512 | bytes 5565655 | solution.py:200
  122.3 14.9 %while.51 = (s32[]{:T(128)}, f32[256,4,64]{0,2,1:T(8,128)}, s32[4,512]{1,0:T(4,128)}, s32[]{:T(128)}, s32[1,256]{1,0:T(1,128)S(1)}, /*index=5*/bf16[4,512,256]{1...) while((s32[]{:T(128)}, f32[256,4,64]{0,2,1:T(8,128)}, ...), condition=%wide.region_12.13_spmd, body=%wide.region_8.0_spmd.sunk | while | flops 136512000 | bytes 2501831 | solution.py:223
  125.0 4.4 conditional.9
  148.8 4.3 fusion.151
  158.9 21.6 %all-to-all-start.3 = ((bf16[8,256,256]{2,1,0:T(8,128)(2,1)}), bf16[8,256,256]{2,1,0:T(8,128)(2,1)S(1)}, u32[]{:S(2)}, u32[]{:S(2)}) async-start(bf16[8,256,256]{2,1,0:T(8,128)(2,1)} %broadcast_in_dim.172), calls=%async_computation.3 | async-start | bytes 2097152 | tf_op jit(solution)/shard_map/all_to_all | solution.py:52
  186.8 5.4 all-gather.6.cloned.1.call-done
  198.2 7.3 %all-to-all-done.3 = bf16[8,256,256]{2,1,0:T(8,128)(2,1)S(1)} async-done(((bf16[8,256,256]{2,1,0:T(8,128)(2,1)}), bf16[8,256,256]{2,1,0:T(8,128)(2,1)S(1)}, u32[]{:S(2)}, u32[]{:S(2)}) %all-to-all-start.3) | async-done | bytes 1048608 | tf_op jit(solution)/shard_map/all_to_all | solution.py:52
  249.6 5.7 %all-to-all-start.7 = ((bf16[8,128,512]{1,2,0:T(8,128)(2,1)}), bf16[8,128,512]{1,2,0:T(8,128)(2,1)}, u32[]{:S(2)}, u32[]{:S(2)}) async-start(bf16[8,128,512]{1,2,0:T(8,128)(2,1)} %pad_maximum_fusion.1), calls=%async_computation.7 | async-start | bytes 2097152 | tf_op jit(solution)/shard_map/all_to_all | solution.py:20
  261.7 16.2 %while.52 = (s32[]{:T(128)}, f32[256,4,64]{0,2,1:T(8,128)}, s32[4,512]{1,0:T(4,128)}, s32[]{:T(128)}, s32[1,256]{1,0:T(1,128)S(1)}, /*index=5*/bf16[4,512,256]{1...) while((s32[]{:T(128)}, f32[256,4,64]{0,2,1:T(8,128)}, ...), condition=%wide.region_33.34_spmd, body=%wide.region_29.33_spmd.sunk | while | flops 204669440 | bytes 7109891 | solution.py:340
  264.3 5.8 %conditional.10 = (f32[256,4,64]{0,2,1:T(8,128)}) conditional(s32[]{:T(128)} %convert_element_type.750, f32[256,4,64]{0,2,1:T(8,128)} %get-tuple-element.1209, (s32[1,512]{1,0:T(1,128)S(1)}, s32[1,256]{1,0:T(1,128)S(1)}, bf16[4,512,256]{1,2,0:T(8,128)(2,1)S(1)}, s32[]{:T(128)}, bf16[256,4,64]{0,2,1:T(8,128)(2,1)S(1)}, ...), branch_computations={%region_31.31_spmd, %region_32.32_spmd} | conditional | flops 204668928 | bytes 7105576 | solution.py:338
  283.8 19.7 %all-to-all-start.5 = ((bf16[8,256,256]{2,1,0:T(8,128)(2,1)}), bf16[8,256,256]{2,1,0:T(8,128)(2,1)S(1)}, u32[]{:S(2)}, u32[]{:S(2)}) async-start(bf16[8,256,256]{2,1,0:T(8,128)(2,1)} %broadcast_in_dim.174), calls=%async_computation.5 | async-start | bytes 2097152 | tf_op jit(solution)/shard_map/all_to_all | solution.py:52
  313.7 15.7 %all-to-all-done.5 = bf16[8,256,256]{2,1,0:T(8,128)(2,1)S(1)} async-done(((bf16[8,256,256]{2,1,0:T(8,128)(2,1)}), bf16[8,256,256]{2,1,0:T(8,128)(2,1)S(1)}, u32[]{:S(2)}, u32[]{:S(2)}) %all-to-all-start.5) | async-done | bytes 1048608 | tf_op jit(solution)/shard_map/all_to_all | solution.py:52
  336.0 4.7 all-to-all-done.6
  340.8 29.2 %while.53 = (s32[]{:T(128)}, f32[256,4,64]{0,2,1:T(8,128)S(1)}, f32[256,4,64]{0,2,1:T(8,128)S(1)}, s32[4,512]{1,0:T(4,128)}, s32[]{:T(128)}, /*index=5*/s32[1,25...) while((s32[]{:T(128)}, f32[256,4,64]{0,2,1:T(8,128)S(1)}, ...), condition=%wide.region_39.40_spmd, body=%wide.region_35.39_spmd.sunk | while | flops 272368128 | bytes 10018075 | solution.py:382
  343.4 4.6 conditional.11
  350.8 4.6 conditional.11
  358.1 4.6 conditional.11
  365.4 4.6 conditional.11
  383.3 55.7 %all_to_all.52 = bf16[8,272,512]{2,1,0:T(8,128)(2,1)S(1)} all-to-all(bf16[8,272,512]{2,1,0:T(8,128)(2,1)} %reshape_reshape.27), channel_id=1, replica_groups=mesh['fsdp'=2,'ctx'=8,'tp'=2] {'ctx'}, dimensions={0} | all-to-all | bytes 4456448 | tf_op jit(solution)/shard_map/all_to_all | solution.py:60
  447.5 71.9 %all-reduce = (f32[4]{0:T(128)S(1)}, f32[1024]{0:T(1024)}) all-reduce(f32[4]{0:T(128)S(1)} %pad_maximum_fusion.7, f32[1024]{0:T(1024)S(1)} %copy-done.88), channel_id=1, replica_groups=mesh['fsdp'=2,'ctx'=8,'tp'=2] {'fsdp','ctx'}, use_global_device_ids=true, to_apply=%region_45.46 | all-reduce | flops 1028 | bytes 8224 | tf_op jit(solution)/shard_map/psum | solution.py:455
  527.5 5.9 %collective-permute-done.5 = bf16[256,512]{1,0:T(8,128)(2,1)S(1)} collective-permute-done((bf16[256,512]{1,0:T(8,128)(2,1)S(1)}, bf16[256,512]{1,0:T(8,128)(2,1)S(1)}, u32[]{:S(2)}, u32[]{:S(2)}) %collective-permute-start.5) | collective-permute-done | bytes 262176 | tf_op jit(solution)/shard_map/ppermute | solution.py:39
  (489 shorter events, 256.5 us)
Async XLA Ops:
  23.6 28.3 %all-to-all-start.2 = ((bf16[8,128,512]{2,1,0:T(8,128)(2,1)}), bf16[8,128,512]{2,1,0:T(8,128)(2,1)S(1)}, u32[]{:S(2)}, u32[]{:S(2)}) async-start(bf16[8,128,512]{2,1,0:T(8,128)(2,1)} %broadcast_in_dim.169), calls=%async_computation.2 | async-start | bytes 2097152 | tf_op jit(solution)/shard_map/all_to_all | solution.py:52
  53.5 52.0 %all-to-all-start.1 = ((bf16[8,256,512]{2,1,0:T(8,128)(2,1)}), bf16[8,256,512]{2,1,0:T(8,128)(2,1)S(1)}, u32[]{:S(2)}, u32[]{:S(2)}) async-start(bf16[8,256,512]{2,1,0:T(8,128)(2,1)} %broadcast_in_dim.165), calls=%async_computation.1 | async-start | bytes 4194304 | tf_op jit(solution)/shard_map/all_to_all | solution.py:52
  57.3 126.8 %all-gather.4.cloned.1.call-start = ((), (), s32[]{:S(2)}) async-start(), calls=%async_computation.10 | async-start | bytes 1572864 | tf_op jit(solution)/shard_map/all_gather | solution.py:144
  140.1 7.1 %collective-permute-start = (bf16[256,512]{1,0:T(8,128)(2,1)S(1)}, bf16[256,512]{1,0:T(8,128)(2,1)S(1)}, u32[]{:S(2)}, u32[]{:S(2)}) collective-permute-start(bf16[256,512]{1,0:T(8,128)(2,1)S(1)} %convolution_convert_fusion.6), channel_id=1, source_target_pairs={{0,1},{1,0},{2,3},{3,2},{4,5},{5,4},{6,7},{7,6},{8,9},{9,8},{10,11... | collective-permute-start | bytes 786440 | tf_op jit(solution)/shard_map/ppermute | solution.py:39
  156.1 25.1 %collective-permute-start.1 = (bf16[256,512]{1,0:T(8,128)(2,1)S(1)}, bf16[256,512]{1,0:T(8,128)(2,1)}, u32[]{:S(2)}, u32[]{:S(2)}) collective-permute-start(bf16[256,512]{1,0:T(8,128)(2,1)S(1)} %convolution_convert_fusion.5), channel_id=1, source_target_pairs={{0,1},{1,0},{2,3},{3,2},{4,5},{5,4},{6,7},{7,6},{8,9},{9,8},{10,11... | collective-permute-start | bytes 786440 | tf_op jit(solution)/shard_map/ppermute | solution.py:39
  158.9 46.7 %all-to-all-start.3 = ((bf16[8,256,256]{2,1,0:T(8,128)(2,1)}), bf16[8,256,256]{2,1,0:T(8,128)(2,1)S(1)}, u32[]{:S(2)}, u32[]{:S(2)}) async-start(bf16[8,256,256]{2,1,0:T(8,128)(2,1)} %broadcast_in_dim.172), calls=%async_computation.3 | async-start | bytes 2097152 | tf_op jit(solution)/shard_map/all_to_all | solution.py:52
  180.5 11.6 %all-gather.6.cloned.1.call-start = ((), (), s32[]{:S(2)}) async-start(), calls=%async_computation.11 | async-start | bytes 1572864 | tf_op jit(solution)/shard_map/all_gather | solution.py:145
  194.9 17.5 %collective-permute-start.2 = (bf16[256,512]{1,0:T(8,128)(2,1)}, bf16[256,512]{1,0:T(8,128)(2,1)}, u32[]{:S(2)}, u32[]{:S(2)}) collective-permute-start(bf16[256,512]{1,0:T(8,128)(2,1)} %convolution_convert_fusion.4), channel_id=1, source_target_pairs={{0,1},{1,0},{2,3},{3,2},{4,5},{5,4},{6,7},{7,6},{8,9},{9,8},{10,11... | collective-permute-start | bytes 786440 | tf_op jit(solution)/shard_map/ppermute | solution.py:39
  208.2 41.4 %all-to-all-start.4 = ((f32[8,256,4]{1,2,0:T(4,128)}), f32[8,256,4]{1,2,0:T(4,128)}, u32[]{:S(2)}, u32[]{:S(2)}) async-start(f32[8,256,4]{1,2,0:T(4,128)} %broadcast_in_dim.173), calls=%async_computation.4 | async-start | bytes 65536 | tf_op jit(solution)/shard_map/all_to_all | solution.py:52
  220.8 7.2 %collective-permute-start.3 = (bf16[256,512]{1,0:T(8,128)(2,1)S(1)}, bf16[256,512]{1,0:T(8,128)(2,1)S(1)}, u32[]{:S(2)}, u32[]{:S(2)}) collective-permute-start(bf16[256,512]{1,0:T(8,128)(2,1)S(1)} %convolution_convert_fusion.3), channel_id=1, source_target_pairs={{0,1},{1,0},{2,3},{3,2},{4,5},{5,4},{6,7},{7,6},{8,9},{9,8},{10,11... | collective-permute-start | bytes 786440 | tf_op jit(solution)/shard_map/ppermute | solution.py:39
  222.9 19.8 %collective-permute-start.13 = (bf16[1024,256]{1,0:T(8,128)(2,1)}, bf16[1024,256]{1,0:T(8,128)(2,1)}, u32[]{:S(2)}, u32[]{:S(2)}) collective-permute-start(bf16[1024,256]{1,0:T(8,128)(2,1)} %dynamic-slice_convert_fusion), channel_id=1, source_target_pairs={{0,16},{16,0},{1,17},{17,1},{2,18},{18,2},{3,19},{19,3},{4,20},{20... | collective-permute-start | bytes 1572872 | tf_op jit(solution)/shard_map/ppermute | solution.py:47
  224.4 21.1 %collective-permute-start.12 = (bf16[256,1024]{1,0:T(8,128)(2,1)}, bf16[256,1024]{1,0:T(8,128)(2,1)}, u32[]{:S(2)}, u32[]{:S(2)}) collective-permute-start(bf16[256,1024]{1,0:T(8,128)(2,1)} %dynamic-slice_convert_fusion.1), channel_id=1, source_target_pairs={{0,16},{16,0},{1,17},{17,1},{2,18},{18,2},{3,19},{19,3},{4,20},{20... | collective-permute-start | bytes 1572872 | tf_op jit(solution)/shard_map/ppermute | solution.py:47
  235.7 11.9 %collective-permute-start.4 = (bf16[256,512]{1,0:T(8,128)(2,1)S(1)}, bf16[256,512]{1,0:T(8,128)(2,1)}, u32[]{:S(2)}, u32[]{:S(2)}) collective-permute-start(bf16[256,512]{1,0:T(8,128)(2,1)S(1)} %convolution_convert_fusion.2), channel_id=1, source_target_pairs={{0,1},{1,0},{2,3},{3,2},{4,5},{5,4},{6,7},{7,6},{8,9},{9,8},{10,11... | collective-permute-start | bytes 786440 | tf_op jit(solution)/shard_map/ppermute | solution.py:39
  249.5 57.0 %collective-permute-start.17 = (bf16[3,256]{1,0:T(4,128)(2,1)}, bf16[3,256]{1,0:T(4,128)(2,1)}, u32[]{:S(2)}, u32[]{:S(2)}) collective-permute-start(bf16[3,256]{1,0:T(4,128)(2,1)} %fusion.115), channel_id=1, source_target_pairs={{0,16},{16,0},{1,17},{17,1},{2,18},{18,2},{3,19},{19,3},{4,20},{20... | collective-permute-start | bytes 4616 | tf_op jit(solution)/shard_map/ppermute | solution.py:47
  249.6 32.2 %all-to-all-start.7 = ((bf16[8,128,512]{1,2,0:T(8,128)(2,1)}), bf16[8,128,512]{1,2,0:T(8,128)(2,1)}, u32[]{:S(2)}, u32[]{:S(2)}) async-start(bf16[8,128,512]{1,2,0:T(8,128)(2,1)} %pad_maximum_fusion.1), calls=%async_computation.7 | async-start | bytes 2097152 | tf_op jit(solution)/shard_map/all_to_all | solution.py:20
  255.9 51.3 %collective-permute-start.16 = (bf16[3,256]{1,0:T(4,128)(2,1)}, bf16[3,256]{1,0:T(4,128)(2,1)}, u32[]{:S(2)}, u32[]{:S(2)}) collective-permute-start(bf16[3,256]{1,0:T(4,128)(2,1)} %fusion.112), channel_id=1, source_target_pairs={{0,16},{16,0},{1,17},{17,1},{2,18},{18,2},{3,19},{19,3},{4,20},{20... | collective-permute-start | bytes 4616 | tf_op jit(solution)/shard_map/ppermute | solution.py:47
  257.1 51.9 %collective-permute-start.15 = (bf16[3,256]{1,0:T(4,128)(2,1)}, bf16[3,256]{1,0:T(4,128)(2,1)}, u32[]{:S(2)}, u32[]{:S(2)}) collective-permute-start(bf16[3,256]{1,0:T(4,128)(2,1)} %fusion.109), channel_id=1, source_target_pairs={{0,16},{16,0},{1,17},{17,1},{2,18},{18,2},{3,19},{19,3},{4,20},{20... | collective-permute-start | bytes 4616 | tf_op jit(solution)/shard_map/ppermute | solution.py:47
  283.8 45.7 %all-to-all-start.5 = ((bf16[8,256,256]{2,1,0:T(8,128)(2,1)}), bf16[8,256,256]{2,1,0:T(8,128)(2,1)S(1)}, u32[]{:S(2)}, u32[]{:S(2)}) async-start(bf16[8,256,256]{2,1,0:T(8,128)(2,1)} %broadcast_in_dim.174), calls=%async_computation.5 | async-start | bytes 2097152 | tf_op jit(solution)/shard_map/all_to_all | solution.py:52
  303.7 6.6 %collective-permute-start.8 = (bf16[256,256]{1,0:T(8,128)(2,1)S(1)}, bf16[256,256]{1,0:T(8,128)(2,1)S(1)}, u32[]{:S(2)}, u32[]{:S(2)}) collective-permute-start(bf16[256,256]{1,0:T(8,128)(2,1)S(1)} %dynamic-slice_convert_fusion.5), channel_id=1, source_target_pairs={{0,16},{16,0},{1,17},{17,1},{2,18},{18,2},{3,19},{19,3},{4,20},{20... | collective-permute-start | bytes 393224 | tf_op jit(solution)/shard_map/ppermute | solution.py:47
  330.1 10.7 %all-to-all-start.6 = ((f32[8,256,4]{1,2,0:T(4,128)}), f32[8,256,4]{1,2,0:T(4,128)}, u32[]{:S(2)}, u32[]{:S(2)}) async-start(f32[8,256,4]{1,2,0:T(4,128)} %broadcast_in_dim.175), calls=%async_computation.6 | async-start | bytes 65536 | tf_op jit(solution)/shard_map/all_to_all | solution.py:52
  334.7 38.9 %collective-permute-start.10 = (bf16[2,256,256]{1,2,0:T(8,128)(2,1)}, bf16[2,256,256]{1,2,0:T(8,128)(2,1)}, u32[]{:S(2)}, u32[]{:S(2)}) collective-permute-start(bf16[2,256,256]{1,2,0:T(8,128)(2,1)} %fusion.72), channel_id=1, source_target_pairs={{0,16},{16,0},{1,17},{17,1},{2,18},{18,2},{3,19},{19,3},{4,20},{20... | collective-permute-start | bytes 786440 | tf_op jit(solution)/shard_map/ppermute | solution.py:47
  441.1 93.2 %all-to-all-start.9 = ((bf16[8,272,512]{2,1,0:T(8,128)(2,1)}), bf16[8,272,512]{2,1,0:T(8,128)(2,1)S(1)}, u32[]{:S(2)}, u32[]{:S(2)}) async-start(bf16[8,272,512]{2,1,0:T(8,128)(2,1)} %broadcast_in_dim.179), calls=%async_computation.9 | async-start | bytes 4456448 | tf_op jit(solution)/shard_map/all_to_all | solution.py:52
  521.2 5.6 collective-permute-start.6
  525.3 8.1 %collective-permute-start.5 = (bf16[256,512]{1,0:T(8,128)(2,1)S(1)}, bf16[256,512]{1,0:T(8,128)(2,1)S(1)}, u32[]{:S(2)}, u32[]{:S(2)}) collective-permute-start(bf16[256,512]{1,0:T(8,128)(2,1)S(1)} %fusion.51), channel_id=1, source_target_pairs={{0,1},{1,0},{2,3},{3,2},{4,5},{5,4},{6,7},{7,6},{8,9},{9,8},{10,11... | collective-permute-start | bytes 786440 | tf_op jit(solution)/shard_map/ppermute | solution.py:39
  (98 other events, 1157.5 us)
Sparse Core Ops, SparseCore 0:
  59.6 10.3 all-gather.3
  182.9 9.2 all-gather.5

commit v2 on v1

--- a/solution.py
+++ b/solution.py
@@ -1,6 +1,8 @@
 import jax
 import jax.numpy as jnp
 from jax import lax
+from jax.experimental import pallas as pl
+from jax.experimental.pallas import tpu as pltpu
 from jax.sharding import PartitionSpec as P
 
 HEAD = 64
@@ -98,22 +100,184 @@
     return (grad_in, jnp.sum(grad_out * normed, axis=0), jnp.sum(grad_out, axis=0))
 
 
-def in_blocks(items):
-    count = items[0].shape[0]
-    width = 512
-    return tuple((item.reshape((count // width, width) + item.shape[1:]) for item in items))
-
-
 def pass_state(state):
     return state
 
 
-def scores_of(query_heads, key_heads, query_segs, key_segs):
-    scores = jnp.einsum(
-        "qhd,khd->qhk", query_heads, key_heads, preferred_element_type=jnp.float32
-    ) * HEAD ** (-0.5)
-    allowed = key_segs[None, None, :] <= query_segs[:, None, None]
-    return jnp.where(allowed, scores, NEG)
+def seg_column(rows):
+    wide = jnp.broadcast_to(rows[:1].astype(jnp.float32), (128, rows.shape[1]))
+    return wide.T[:, :1]
+
+
+def turned(block):
+    return block.astype(jnp.float32).T.astype(jnp.bfloat16)
+
+
+def attend_kernel(low_ref, high_ref, q_ref, kv_ref, o_ref, stat_ref, key_ref, seg_ref):
+    step = pl.program_id(0)
+    chunks = kv_ref.shape[0]
+    width = kv_ref.shape[2]
+
+    @pl.when(step == 0)
+    def _():
+        @pl.loop(0, chunks)
+        def _(j):
+            key_ref[j] = turned(kv_ref[j, :HEAD])
+            seg_ref[j] = seg_column(kv_ref[j, 2 * HEAD :])
+
+    queries = (q_ref[0, :HEAD].astype(jnp.float32) * HEAD ** (-0.5)).astype(jnp.bfloat16)
+    own_seg = q_ref[0, 3 * HEAD :][:1].astype(jnp.float32)
+    top = high_ref[step]
+
+    def one(j, state):
+        def compute(state):
+            row_max, row_sum, total = state
+            scores = matmul(key_ref[j], queries)
+            scores = jnp.where(seg_ref[j] <= own_seg, scores, NEG)
+            new_max = jnp.maximum(row_max, jnp.max(scores, axis=0, keepdims=True))
+            keep = jnp.exp(row_max - new_max)
+            powers = jnp.exp(scores - new_max)
+            row_sum = row_sum * keep + jnp.sum(powers, axis=0, keepdims=True)
+            total = total * keep + matmul(kv_ref[j, HEAD : 2 * HEAD], powers.astype(jnp.bfloat16))
+            return (new_max, row_sum, total)
+
+        return lax.cond(low_ref[j] <= top, compute, pass_state, state)
+
+    start = (
+        jnp.full((1, width), NEG, jnp.float32),
+        jnp.zeros((1, width), jnp.float32),
+        jnp.zeros((HEAD, width), jnp.float32),
+    )
+    row_max, row_sum, total = lax.fori_loop(0, chunks, one, start)
+    o_ref[0] = total / row_sum
+    stat_ref[0] = row_max + jnp.log(row_sum)
+
+
+def attend_back_kernel(
+    low_ref, high_ref, q_ref, kv_ref, g_ref, o_ref, stat_ref, dq_ref, dkv_ref, key_ref, val_ref, seg_ref
+):
+    step = pl.program_id(0)
+    chunks = kv_ref.shape[0]
+    width = kv_ref.shape[2]
+
+    @pl.when(step == 0)
+    def _():
+        @pl.loop(0, chunks)
+        def _(j):
+            key_ref[j] = turned(kv_ref[j, :HEAD])
+            val_ref[j] = turned(kv_ref[j, HEAD : 2 * HEAD])
+            seg_ref[j] = seg_column(kv_ref[j, 2 * HEAD :])
+            dkv_ref[j] = jnp.zeros(dkv_ref.shape[1:], jnp.float32)
+
+    queries = (q_ref[0, :HEAD].astype(jnp.float32) * HEAD ** (-0.5)).astype(jnp.bfloat16)
+    own_seg = q_ref[0, 3 * HEAD :][:1].astype(jnp.float32)
+    grads = g_ref[0]
+    delta = jnp.sum(grads.astype(jnp.float32) * o_ref[0], axis=0, keepdims=True)
+    log_sum = stat_ref[0]
+    top = high_ref[step]
+
+    def one(j, total):
+        def compute(total):
+            scores = matmul(key_ref[j], queries)
+            scores = jnp.where(seg_ref[j] <= own_seg, scores, NEG)
+            probs = jnp.exp(scores - log_sum)
+            grad_probs = matmul(val_ref[j], grads)
+            grad_scores = (probs * (grad_probs - delta)).astype(jnp.bfloat16)
+            dkv_ref[j, :HEAD] += matmul_nt(queries, grad_scores)
+            dkv_ref[j, HEAD:] += matmul_nt(grads, probs.astype(jnp.bfloat16))
+            return total + matmul(kv_ref[j, :HEAD], grad_scores)
+
+        return lax.cond(low_ref[j] <= top, compute, pass_state, total)
+
+    total = lax.fori_loop(0, chunks, one, jnp.zeros((HEAD, width), jnp.float32))
+    dq_ref[0] = (total * HEAD ** (-0.5)).astype(jnp.bfloat16)
+
+
+def whole(shape):
+    return pl.BlockSpec(shape, lambda i, *_: (0,) * len(shape))
+
+
+def by_step(shape):
+    return pl.BlockSpec((1,) + shape[1:], lambda i, *_: (i,) + (0,) * (len(shape) - 1))
+
+
+def attend(low, high, own, kv):
+    count, _, width = own.shape
+    chunks = kv.shape[0]
+    outs = (
+        jax.ShapeDtypeStruct((count, HEAD, width), jnp.float32),
+        jax.ShapeDtypeStruct((count, 1, width), jnp.float32),
+    )
+    pairs = count * chunks * width * width
+    return pl.pallas_call(
+        attend_kernel,
+        out_shape=outs,
+        grid_spec=pltpu.PrefetchScalarGridSpec(
+            num_scalar_prefetch=2,
+            grid=(count,),
+            in_specs=[by_step(own.shape), whole(kv.shape)],
+            out_specs=[by_step(o.shape) for o in outs],
+            scratch_shapes=[
+                pltpu.VMEM((chunks, width, HEAD), jnp.bfloat16),
+                pltpu.VMEM((chunks, width, 1), jnp.float32),
+            ],
+        ),
+        cost_estimate=pl.CostEstimate(
+            flops=2 * HEAD * pairs, transcendentals=pairs // 2, bytes_accessed=kv.size * 2
+        ),
+        name="attend",
+    )(low, high, own, kv)
+
+
+def attend_back(low, high, own, kv, grads, mixed, log_sum):
+    count, _, width = own.shape
+    chunks = kv.shape[0]
+    outs = (
+        jax.ShapeDtypeStruct((count, HEAD, width), jnp.bfloat16),
+        jax.ShapeDtypeStruct((chunks, 2 * HEAD, width), jnp.float32),
+    )
+    pairs = count * chunks * width * width
+    return pl.pallas_call(
+        attend_back_kernel,
+        out_shape=outs,
+        grid_spec=pltpu.PrefetchScalarGridSpec(
+            num_scalar_prefetch=2,
+            grid=(count,),
+            in_specs=[
+                by_step(own.shape),
+                whole(kv.shape),
+                by_step(grads.shape),
+                by_step(mixed.shape),
+                by_step(log_sum.shape),
+            ],
+            out_specs=[by_step(outs[0].shape), whole(outs[1].shape)],
+            scratch_shapes=[
+                pltpu.VMEM((chunks, width, HEAD), jnp.bfloat16),
+                pltpu.VMEM((chunks, width, HEAD), jnp.bfloat16),
+                pltpu.VMEM((chunks, width, 1), jnp.float32),
+            ],
+        ),
+        cost_estimate=pl.CostEstimate(
+            flops=5 * HEAD * pairs, transcendentals=pairs // 2, bytes_accessed=kv.size * 8
+        ),
+        name="attend_back",
+    )(low, high, own, kv, grads, mixed, log_sum)
+
+
+def head_groups(heads):
+    members = lax.axis_size("ctx") // heads
+    return [[head * members + m for head in range(heads)] for m in range(members)]
+
+
+def to_heads(pieces):
+    groups = head_groups(pieces.shape[0])
+    return lax.all_to_all(pieces, "ctx", 0, 0, axis_index_groups=groups, tiled=True)
+
+
+def member_shift(heads, shift):
+    size = lax.axis_size("ctx")
+    members = size // heads
+    return [(i, i // members * members + (i + shift) % members) for i in range(size)]
 
 
 def per_device(
@@ -160,78 +324,33 @@
     def head_total(partial_value):
         return tp_total(partial_value.astype(jnp.bfloat16))
 
+    def over_ctx(x):
+        stacked = gather_by_exchange(x, "ctx")
+        return stacked.reshape((-1,) + x.shape[1:])
+
     inputs = tokens[0]
     resid_in = inputs.astype(jnp.float32)
     query_segs = block_ids[0]
-    top_seg = jnp.max(query_segs)
-    low_seg = jnp.min(query_segs)
     rows = inputs.shape[0]
-    queries = (matmul(inputs, w_qkv[0]) + b_attn[0]).astype(jnp.bfloat16)
-    keys = matmul(inputs, w_qkv[1]).astype(jnp.bfloat16)
-    values = (matmul(inputs, w_qkv[2]) + b_attn[1]).astype(jnp.bfloat16)
-    query_heads = split_heads(queries)
-    key_heads = split_heads(keys)
-    value_heads = split_heads(values)
-    heads = query_heads.shape[1]
-    start_state = (jnp.full((rows, heads), NEG, jnp.float32), jnp.zeros((rows, heads), jnp.float32))
-    empty_heads = jnp.zeros((rows, heads, HEAD), jnp.float32)
-
-    def over_ctx(x):
-        stacked = gather_by_exchange(x, "ctx")
-        return stacked.reshape((-1,) + x.shape[1:])
-
-    both = over_ctx(jnp.concatenate([keys, values], axis=1))
-    all_keys, all_values = both[:, : keys.shape[1]], both[:, keys.shape[1] :]
-    all_segs = over_ctx(query_segs)
-
-    def stat_one_block(inner, block):
-
-        def stat_compute(current):
-            row_max, row_sum = current
-            scores = scores_of(query_heads, split_heads(block[0]), query_segs, block[1])
-            new_max = jnp.maximum(row_max, jnp.max(scores, axis=-1))
-            total = row_sum * jnp.exp(row_max - new_max) + jnp.sum(
-                jnp.exp(scores - new_max[..., None]), axis=-1
-            )
-            return (new_max, total)
-
-        return (lax.cond(jnp.min(block[1]) <= top_seg, stat_compute, pass_state, inner), None)
-
-    row_max, row_sum = lax.scan(
-        stat_one_block,
-        start_state,
-        in_blocks(
-            (
-                all_keys,
-                all_segs,
-            )
-        ),
-    )[0]
-    log_sum = row_max + jnp.log(row_sum)
-
-    def out_one_block(inner, block):
-
-        def out_compute(current):
-            scores = scores_of(query_heads, split_heads(block[0]), query_segs, block[2])
-            weights = jnp.exp(scores - log_sum[..., None]).astype(jnp.bfloat16)
-            return current + jnp.einsum(
-                "qhk,khd->qhd", weights, split_heads(block[1]), preferred_element_type=jnp.float32
-            )
-
-        return (lax.cond(jnp.min(block[2]) <= top_seg, out_compute, pass_state, inner), None)
-
-    mixed = lax.scan(
-        out_one_block,
-        empty_heads,
-        in_blocks(
-            (
-                all_keys,
-                all_values,
-                all_segs,
-            )
-        ),
-    )[0]
-    mixed_low = mixed.reshape(rows, -1).astype(jnp.bfloat16)
+    local_heads = w_qkv.shape[2] // HEAD
+    shift_v = jnp.stack([b_attn[0], jnp.zeros_like(b_attn[0]), b_attn[1]])
+    packed = lax.dot_general(w_qkv, inputs, (((1,), (1,)), ((), ())), preferred_element_type=jnp.float32)
+    packed = (packed + shift_v[:, :, None]).astype(jnp.bfloat16)
+    packed = packed.reshape(3, local_heads, HEAD, rows).swapaxes(0, 1)
+    packed = packed.reshape(local_heads, 3 * HEAD, rows)
+    seg_rows = jnp.broadcast_to(query_segs.astype(jnp.bfloat16), (local_heads, 16, rows))
+    own = to_heads(jnp.concatenate([packed, seg_rows], axis=1))
+    members = lax.axis_size("ctx") // local_heads
+    rounds = tuple(range(1, members))
+    own_kv = own[:, HEAD:]
+    kv = jnp.concatenate(
+        [own_kv] + [lax.ppermute(own_kv, "ctx", member_shift(local_heads, -s)) for s in rounds]
+    )
+    low = kv[:, 2 * HEAD, 0].astype(jnp.int32)
+    high = kv[:local_heads, 2 * HEAD, rows - 1].astype(jnp.int32)
+    head_out, log_sum = attend(low, high, own, kv)
+    mixed_t = to_heads(head_out.astype(jnp.bfloat16)).reshape(-1, rows)
+    mixed_low = mixed_t.T
     self_branch = head_total(matmul(mixed_low, w_out)) + b_out[0]
     first, first_norm, first_inv = norm_forward(resid_in + self_branch, gains[0], shifts[0])
     first_low = first.astype(jnp.bfloat16)
@@ -318,82 +437,15 @@
     )
     grad_self_low = grad_first.astype(jnp.bfloat16)
     grad_mixed = matmul_nt(grad_self_low, w_out).astype(jnp.bfloat16)
-    gm_heads = split_heads(grad_mixed)
-    delta = jnp.sum(gm_heads.astype(jnp.float32) * mixed, axis=-1)
-
-    def query_one_block(inner, block):
-
-        def query_compute(current):
-            block_keys = split_heads(block[0])
-            scores = scores_of(query_heads, block_keys, query_segs, block[2])
-            probs = jnp.exp(scores - log_sum[..., None])
-            grad_probs = jnp.einsum(
-                "qhd,khd->qhk", gm_heads, split_heads(block[1]), preferred_element_type=jnp.float32
-            )
-            grad_scores = (probs * (grad_probs - delta[..., None])).astype(jnp.bfloat16)
-            return current + jnp.einsum(
-                "qhk,khd->qhd", grad_scores, block_keys, preferred_element_type=jnp.float32
-            )
-
-        return (lax.cond(jnp.min(block[2]) <= top_seg, query_compute, pass_state, inner), None)
-
-    grad_q_sum = lax.scan(
-        query_one_block,
-        empty_heads,
-        in_blocks(
-            (
-                all_keys,
-                all_values,
-                all_segs,
-            )
-        ),
-    )[0]
-    all_log_sum, all_delta = (
-        over_ctx(log_sum),
-        over_ctx(delta),
-    )
-
-    def key_one_block(inner, block):
-        remote_q, remote_grad, remote_segs, block_sum, block_delta = block
-
-        def key_compute(current):
-            grad_key_sum, grad_value_sum = current
-            remote_heads = split_heads(remote_q)
-            remote_grads = split_heads(remote_grad)
-            scores = scores_of(remote_heads, key_heads, remote_segs, query_segs)
-            probs = jnp.exp(scores - block_sum[..., None])
-            grad_value_sum = grad_value_sum + jnp.einsum(
-                "qhk,qhd->khd",
-                probs.astype(jnp.bfloat16),
-                remote_grads,
-                preferred_element_type=jnp.float32,
-            )
-            grad_probs = jnp.einsum(
-                "qhd,khd->qhk", remote_grads, value_heads, preferred_element_type=jnp.float32
-            )
-            grad_scores = (probs * (grad_probs - block_delta[..., None])).astype(jnp.bfloat16)
-            grad_key_sum = grad_key_sum + jnp.einsum(
-                "qhk,qhd->khd", grad_scores, remote_heads, preferred_element_type=jnp.float32
-            )
-            return (grad_key_sum, grad_value_sum)
-
-        return (lax.cond(jnp.max(remote_segs) >= low_seg, key_compute, pass_state, inner), None)
-
-    grad_k_sum, grad_v_sum = lax.scan(
-        key_one_block,
-        (empty_heads, empty_heads),
-        in_blocks(
-            (
-                over_ctx(queries),
-                over_ctx(grad_mixed),
-                all_segs,
-            )
-            + (all_log_sum, all_delta)
-        ),
-    )[0]
-    grad_q = (grad_q_sum * HEAD ** (-0.5)).reshape(rows, -1).astype(jnp.bfloat16)
-    grad_k = (grad_k_sum * HEAD ** (-0.5)).reshape(rows, -1).astype(jnp.bfloat16)
-    grad_v = grad_v_sum.reshape(rows, -1).astype(jnp.bfloat16)
+    grads_in = to_heads(grad_mixed.T.reshape(local_heads, HEAD, rows))
+    part_q, part_kv = attend_back(low, high, own, kv, grads_in, head_out, log_sum)
+    sum_kv = part_kv[:local_heads]
+    for s in rounds:
+        away = part_kv[s * local_heads : (s + 1) * local_heads].astype(jnp.bfloat16)
+        sum_kv = sum_kv + lax.ppermute(away, "ctx", member_shift(local_heads, s)).astype(jnp.float32)
+    back = to_heads(jnp.concatenate([part_q, sum_kv.astype(jnp.bfloat16)], axis=1))
+    back = back.reshape(local_heads, 3, HEAD, rows).swapaxes(0, 1).reshape(3, -1, rows)
+    grad_q, grad_k, grad_v = back[0].T, back[1].T, back[2].T
     input_part = (
         matmul_nt(grad_q, w_qkv[0]) + matmul_nt(grad_k, w_qkv[1]) + matmul_nt(grad_v, w_qkv[2])
     )
@@ -432,9 +484,21 @@
         (g_gain, 1),
         (g_shift, 1),
     )
+    squares = jnp.stack(
+        [
+            jnp.sum(resid_in * resid_in),
+            jnp.sum(self_branch * self_branch),
+            jnp.sum(cross_branch * cross_branch),
+            jnp.sum(ffn_branch * ffn_branch),
+        ]
+    )
+    square_high = squares.astype(jnp.bfloat16)
+    square_low = (squares - square_high.astype(jnp.float32)).astype(jnp.bfloat16)
+    extra = jnp.concatenate([g_fbias.astype(jnp.bfloat16), square_high, square_low])
     halves = [pair_scatter(g, dim) for g, dim in big]
     flats = [h.astype(jnp.bfloat16).reshape(-1) for h in halves]
     size = lax.axis_size("ctx")
+    flats.append(extra)
     lengths = [f.shape[0] for f in flats]
     pad = -sum(lengths) % (512 * 16 * size)
     packed = jnp.concatenate(flats + [jnp.zeros((pad,), jnp.bfloat16)]).reshape(-1, 512)
@@ -444,15 +508,10 @@
         outs.append(summed[at : at + length].reshape(h.shape))
         at += length
     o_qkv, o_out, o_cq, o_ckv, o_co, o_fin, o_fout, o_abias, o_obias, o_gain, o_shift = outs
-    squares = jnp.stack(
-        [
-            jnp.sum(resid_in * resid_in),
-            jnp.sum(self_branch * self_branch),
-            jnp.sum(cross_branch * cross_branch),
-            jnp.sum(ffn_branch * ffn_branch),
-        ]
-    )
-    fbias_total, square_total = lax.psum((g_fbias, squares), ("fsdp", "ctx"))
+    extra_sum = summed[at : at + lengths[-1]]
+    extra_sum = extra_sum + lax.ppermute(extra_sum, "fsdp", other("fsdp"))
+    fbias_total = extra_sum[:-8]
+    square_total = extra_sum[-8:-4] + extra_sum[-4:]
     entries = rows * inputs.shape[1] * lax.axis_size("fsdp") * lax.axis_size("ctx")
     rms_values = jnp.sqrt(square_total / entries)
     return (

time: 565 us -> 435 us (0.77)
  blocking collectives: 164 us -> 73.5 us
  starting transfers between devices: 76.2 us -> 48.8 us
  waiting for transfers between devices: 90.9 us -> 116 us
  Pallas kernels: 0 us -> 24.4 us
  loops' own time: 20.6 us -> 0 us
  matrix products: 52.4 us -> 32.5 us
  other arithmetic: 62.2 us -> 44.1 us
    psum x1 -> x0, blocking collectives: 71.9 us -> none  [per_device(): fbias_total, square_total = lax.psum((g_fbias, squares), ('fsdp', 'ctx'))]
    all_to_all x7 -> x2, starting transfers between devices: 60.4 us -> 8.82 us  [gather_by_exchange(): lax.all_to_all(jnp.broadcast_to(x[None], (size,) + x.shape), axis, split_...]
    pallas_call x0 -> x2, Pallas kernels: none -> 24.4 us  [the longest x1 12.4 us: attend_back(): pl.pallas_call(attend_back_kernel, out_shape=outs, grid_spec=pltpu.Prefet...]
    concatenate x1, local copies, waits for them, and re-layouts: 1.19 us -> 24.8 us  [per_device(): jnp.concatenate(flats + [jnp.zeros((pad,), jnp.bfloat16)]).reshape(-1, 512)]
    all_to_all x0 -> x4, waiting for transfers between devices: none -> 21 us  [to_heads(): lax.all_to_all(pieces, 'ctx', 0, 0, axis_index_groups=groups, tiled=True)]
    another operation x20 -> x0, loops' own time: 20.6 us -> none  [the longest x1 5.3 us: per_device(): lax.scan(key_one_block, (empty_heads, empty_heads), in_blocks((over_ctx(q...]
    all_to_all x0 -> x4, starting transfers between devices: none -> 19 us  [to_heads(): lax.all_to_all(pieces, 'ctx', 0, 0, axis_index_groups=groups, tiled=True)]
    reduce_min x13 -> x0, other arithmetic: 16.9 us -> none  [the longest x4 5.48 us: out_one_block(): jnp.min(block[2]) <= top_seg]
  transfers between devices with their start and end apart: 28 -> 30, of which waited for: 11 -> 15; matrix products, arithmetic and copies ran while one was open for 27% -> 23% of each run, Pallas kernels for 0% -> 6%
where the time goes in v2:
time: 435 us; the launch traced here: 430 us
  waiting for transfers between devices  116 us (27%)
  local copies, waits for them, and re-layouts  75.6 us (17%)
  blocking collectives  73.5 us (17%)
  starting transfers between devices  48.8 us (11%)
  other arithmetic  44.1 us (10%)
  matrix products  32.5 us (7%)
  Pallas kernels  24.4 us (6%)
  between operations  15.7 us (4%)
    all_to_all x1, blocking collectives, ctx_total(): lax.all_to_all(pieces, 'ctx', split_axis=0, concat_axis=0, tiled=True)  55.4 us
    all_to_all x2, waiting for transfers between devices, gather_by_exchange(): lax.all_to_all(jnp.broadcast_to(x[None], (size,) + x.shape), axis, split_...  49.3 us
    concatenate x1, local copies, waits for them, and re-layouts, per_device(): jnp.concatenate(flats + [jnp.zeros((pad,), jnp.bfloat16)]).reshape(-1, 512)  24.8 us
    all_to_all x4, waiting for transfers between devices, to_heads(): lax.all_to_all(pieces, 'ctx', 0, 0, axis_index_groups=groups, tiled=True)  21 us
    ppermute x7, waiting for transfers between devices, tp_total(): lax.ppermute(part, 'tp', other('tp')).astype(jnp.float32)  20.2 us
    all_to_all x1, waiting for transfers between devices, sum_at_owner(): lax.all_to_all(pieces, axis, split_axis=0, concat_axis=0, tiled=True)  19.9 us
    all_to_all x4, starting transfers between devices, to_heads(): lax.all_to_all(pieces, 'ctx', 0, 0, axis_index_groups=groups, tiled=True)  19 us
    unnamed x138, local copies, waits for them, and re-layouts  12.6 us
  transfers between devices with their start and end apart: 30, of which 15 were waited for; matrix products, arithmetic and copies ran while one was open for 23% of the time, Pallas kernels for 6%

profile of v2, /device:TPU:0, one launch (start us, length us, event | category | flops | bytes accessed | tf_op | source)
XLA Modules:
  0.0 430.3 jit_solution(17400858635549125106)
XLA Ops:
  17.2 6.2 %all-to-all-start = ((bf16[4,208,256]{2,1,0:T(8,128)(2,1)}), bf16[4,208,256]{2,1,0:T(8,128)(2,1)S(1)}, u32[]{:S(2)}, u32[]{:S(2)}) async-start(bf16[4,208,256]{2,1,0:T(8,128)(2,1)} %pad_maximum_fusion.3), calls=%async_computation | async-start | bytes 851968 | tf_op jit(solution)/shard_map/all_to_all | solution.py:274
  32.9 3.2 all-to-all-done.q_ref
  45.9 12.0 %attend.1 = (f32[4,64,256]{2,1,0:T(8,128)}, f32[4,1,256]{2,1,0:T(1,128)}) custom-call(s32[8]{0:T(128)} %convert_reduce_fusion.5.low_ref, s32[4]{0:T(128)} %fusion.81.high_ref, bf16[4,208,256]{2,1,0:T(8,128)(2,1)} %copy-done.19, bf16[8,144,256]{2,1,0:T(8,128)(2,1)} %pad_maximum_fusion.2.kv_ref), custom_call_target="tpu_custom_call" | custom-call | flops 268435456 | bytes 589824 | tf_op jit(solution)/shard_map/attend/pallas_call | solution.py:212
  59.6 3.3 all-to-all-start.1
  63.5 5.3 %all-to-all-done.1 = bf16[4,64,256]{2,1,0:T(8,128)(2,1)S(1)} async-done(((bf16[4,64,256]{2,1,0:T(8,128)(2,1)}), bf16[4,64,256]{2,1,0:T(8,128)(2,1)S(1)}, u32[]{:S(2)}, u32[]{:S(2)}) %all-to-all-start.1) | async-done | bytes 131104 | tf_op jit(solution)/shard_map/all_to_all | solution.py:274
  69.9 4.8 %all-to-all-start.2 = ((bf16[8,128,512]{2,1,0:T(8,128)(2,1)}), bf16[8,128,512]{2,1,0:T(8,128)(2,1)S(1)}, u32[]{:S(2)}, u32[]{:S(2)}) async-start(bf16[8,128,512]{2,1,0:T(8,128)(2,1)} %broadcast_in_dim.28), calls=%async_computation.2 | async-start | bytes 2097152 | tf_op jit(solution)/shard_map/all_to_all | solution.py:54
  84.8 13.3 %all-to-all-done.2 = bf16[8,128,512]{2,1,0:T(8,128)(2,1)S(1)} async-done(((bf16[8,128,512]{2,1,0:T(8,128)(2,1)}), bf16[8,128,512]{2,1,0:T(8,128)(2,1)S(1)}, u32[]{:S(2)}, u32[]{:S(2)}) %all-to-all-start.2) | async-done | bytes 1048608 | tf_op jit(solution)/shard_map/all_to_all | solution.py:54
  100.7 4.5 %fusion.112 = (f32[256,4]{0,1:T(4,128)S(1)}, f32[256,4,1024]{0,2,1:T(8,128)}) fusion(pred[1024]{0:T(1024)(128)(4,1)} %iota_compare_fusion, bf16[1024,4,64]{0,2,1:T(8,128)(2,1)S(1)} %bitcast.247, bf16[256,4,64]{0,2,1:T(8,128)(2,1)} %bitcast.273), kind=kOutput, calls=%fused_computation.235 | convolution fusion | flops 138413056 | bytes 4854784 | tf_op jit(solution)/shard_map/sub | solution.py:370
  109.8 4.8 %collective-permute-done.2 = bf16[256,512]{1,0:T(8,128)(2,1)S(1)} collective-permute-done((bf16[256,512]{1,0:T(8,128)(2,1)S(1)}, bf16[256,512]{1,0:T(8,128)(2,1)S(1)}, u32[]{:S(2)}, u32[]{:S(2)}) %collective-permute-start.2) | collective-permute-done | bytes 262176 | tf_op jit(solution)/shard_map/ppermute | solution.py:41
  121.5 5.4 %collective-permute-done.3 = bf16[256,512]{1,0:T(8,128)(2,1)} collective-permute-done((bf16[256,512]{1,0:T(8,128)(2,1)S(1)}, bf16[256,512]{1,0:T(8,128)(2,1)}, u32[]{:S(2)}, u32[]{:S(2)}) %collective-permute-start.3) | collective-permute-done | bytes 262176 | tf_op jit(solution)/shard_map/ppermute | solution.py:41
  141.1 3.2 subtract_convert_fusion
  166.5 5.4 %all-to-all-start.3 = ((bf16[4,64,256]{2,1,0:T(8,128)(2,1)}), bf16[4,64,256]{2,1,0:T(8,128)(2,1)S(1)}, u32[]{:S(2)}, u32[]{:S(2)}) async-start(bf16[4,64,256]{2,1,0:T(8,128)(2,1)} %bitcast.36), calls=%async_computation.3 | async-start | bytes 262144 | tf_op jit(solution)/shard_map/all_to_all | solution.py:274
  172.1 5.8 %all-to-all-done.3.g_ref = bf16[4,64,256]{2,1,0:T(8,128)(2,1)S(1)} async-done(((bf16[4,64,256]{2,1,0:T(8,128)(2,1)}), bf16[4,64,256]{2,1,0:T(8,128)(2,1)S(1)}, u32[]{:S(2)}, u32[]{:S(2)}) %all-to-all-start.3) | async-done | bytes 131104 | tf_op jit(solution)/shard_map/all_to_all | solution.py:274
  178.6 12.4 %attend_back.1 = (bf16[4,64,256]{2,1,0:T(8,128)(2,1)}, f32[8,128,256]{2,1,0:T(8,128)}) custom-call(s32[8]{0:T(128)} %convert_reduce_fusion.5.low_ref, s32[4]{0:T(128)} %fusion.81.high_ref, bf16[4,208,256]{2,1,0:T(8,128)(2,1)} %copy-done.19, bf16[8,144,256]{2,1,0:T(8,128)(2,1)} %pad_maximum_fusion.2.kv_ref, bf16[4,64,256]{2,1,0:T(8,128)(2,1)} %copy-done.33, ...), custom_call_target="tpu_custom_call" | custom-call | flops 671088640 | bytes 2359296 | tf_op jit(solution)/shard_map/attend_back/pallas_call | solution.py:240
  196.4 2.9 collective-permute-done.6
  202.3 4.1 all-to-all-start.4
  212.5 6.6 %all-to-all-done.4 = bf16[4,192,256]{2,1,0:T(8,128)(2,1)} async-done(((bf16[4,192,256]{2,1,0:T(8,128)(2,1)}), bf16[4,192,256]{2,1,0:T(8,128)(2,1)}, u32[]{:S(2)}, u32[]{:S(2)}) %all-to-all-start.4) | async-done | bytes 393248 | tf_op jit(solution)/shard_map/all_to_all | solution.py:274
  219.1 4.2 all-to-all-start.5
  229.3 19.9 %all-to-all-done.5 = bf16[8,128,512]{1,2,0:T(8,128)(2,1)} async-done(((bf16[8,128,512]{1,2,0:T(8,128)(2,1)}), bf16[8,128,512]{1,2,0:T(8,128)(2,1)}, u32[]{:S(2)}, u32[]{:S(2)}) %all-to-all-start.5) | async-done | bytes 1048608 | tf_op jit(solution)/shard_map/all_to_all | solution.py:22
  259.2 24.8 %concatenate.20 = bf16[1114112]{0:T(1024)(128)(2,1)S(1)} concatenate(bf16[196608]{0:T(1024)(128)(2,1)} %bitcast.252, bf16[65536]{0:T(1024)(128)(2,1)} %bitcast.268, bf16[65536]{0:T(1024)(128)(2,1)} %bitcast.267, bf16[131072]{0:T(1024)(128)(2,1)S(1)} %bitcast.262, bf16[65536]{0:T(1024)(128)(2,1)} %bitcast.266, bf16[262144]{0:T(1024)(128)(2,1)} %bitcast.242, ...), dimensions={0} | concatenate | bytes 4456448 | tf_op jit(solution)/shard_map/concatenate | solution.py:504
  286.7 55.4 %all_to_all.40 = bf16[8,272,512]{2,1,0:T(8,128)(2,1)S(1)} all-to-all(bf16[8,272,512]{2,1,0:T(8,128)(2,1)} %reshape_reshape.4), channel_id=1, replica_groups=mesh['fsdp'=2,'ctx'=8,'tp'=2] {'ctx'}, dimensions={0} | all-to-all | bytes 4456448 | tf_op jit(solution)/shard_map/all_to_all | solution.py:62
  344.1 4.0 all-to-all-start.7
  354.5 5.8 %collective-permute-done.7 = bf16[256,512]{1,0:T(8,128)(2,1)S(1)} collective-permute-done((bf16[256,512]{1,0:T(8,128)(2,1)S(1)}, bf16[256,512]{1,0:T(8,128)(2,1)S(1)}, u32[]{:S(2)}, u32[]{:S(2)}) %collective-permute-start.7) | collective-permute-done | bytes 262176 | tf_op jit(solution)/shard_map/ppermute | solution.py:41
  362.5 36.0 %all-to-all-done.7 = bf16[8,272,512]{2,1,0:T(8,128)(2,1)S(1)} async-done(((bf16[8,272,512]{2,1,0:T(8,128)(2,1)}), bf16[8,272,512]{2,1,0:T(8,128)(2,1)S(1)}, u32[]{:S(2)}, u32[]{:S(2)}) %all-to-all-start.7) | async-done | bytes 2228256 | tf_op jit(solution)/shard_map/all_to_all | solution.py:54
  (335 shorter events, 160.9 us)
Async XLA Ops:
  17.2 18.9 %all-to-all-start = ((bf16[4,208,256]{2,1,0:T(8,128)(2,1)}), bf16[4,208,256]{2,1,0:T(8,128)(2,1)S(1)}, u32[]{:S(2)}, u32[]{:S(2)}) async-start(bf16[4,208,256]{2,1,0:T(8,128)(2,1)} %pad_maximum_fusion.3), calls=%async_computation | async-start | bytes 851968 | tf_op jit(solution)/shard_map/all_to_all | solution.py:274
  23.4 92.4 %all-gather.4.cloned.1.call-start = ((), (), s32[]{:S(2)}) async-start(), calls=%async_computation.8 | async-start | bytes 1572864 | tf_op jit(solution)/shard_map/all_gather | solution.py:308
  36.1 8.1 %collective-permute-start = (bf16[4,144,256]{2,1,0:T(8,128)(2,1)S(1)}, bf16[4,144,256]{2,1,0:T(8,128)(2,1)S(1)}, u32[]{:S(2)}, u32[]{:S(2)}) collective-permute-start(bf16[4,144,256]{2,1,0:T(8,128)(2,1)S(1)} %slice.205), channel_id=1, source_target_pairs={{0,2},{2,0},{4,6},{6,4},{8,10},{10,8},{12,14},{14,12},{1,3},{3,1},... | collective-permute-start | bytes 884744 | tf_op jit(solution)/shard_map/ppermute | solution.py:347
  59.6 9.2 %all-to-all-start.1 = ((bf16[4,64,256]{2,1,0:T(8,128)(2,1)}), bf16[4,64,256]{2,1,0:T(8,128)(2,1)S(1)}, u32[]{:S(2)}, u32[]{:S(2)}) async-start(bf16[4,64,256]{2,1,0:T(8,128)(2,1)} %convert_element_type.388), calls=%async_computation.1 | async-start | bytes 262144 | tf_op jit(solution)/shard_map/all_to_all | solution.py:274
  69.9 28.3 %all-to-all-start.2 = ((bf16[8,128,512]{2,1,0:T(8,128)(2,1)}), bf16[8,128,512]{2,1,0:T(8,128)(2,1)S(1)}, u32[]{:S(2)}, u32[]{:S(2)}) async-start(bf16[8,128,512]{2,1,0:T(8,128)(2,1)} %broadcast_in_dim.28), calls=%async_computation.2 | async-start | bytes 2097152 | tf_op jit(solution)/shard_map/all_to_all | solution.py:54
  74.7 42.9 %all-gather.6.cloned.1.call-start = ((), (), s32[]{:S(2)}) async-start(), calls=%async_computation.9 | async-start | bytes 1572864 | tf_op jit(solution)/shard_map/all_gather | solution.py:309
  119.3 7.6 %collective-permute-start.3 = (bf16[256,512]{1,0:T(8,128)(2,1)S(1)}, bf16[256,512]{1,0:T(8,128)(2,1)}, u32[]{:S(2)}, u32[]{:S(2)}) collective-permute-start(bf16[256,512]{1,0:T(8,128)(2,1)S(1)} %convolution_convert_fusion.4), channel_id=1, source_target_pairs={{0,1},{1,0},{2,3},{3,2},{4,5},{5,4},{6,7},{7,6},{8,9},{9,8},{10,11... | collective-permute-start | bytes 786440 | tf_op jit(solution)/shard_map/ppermute | solution.py:41
  137.0 7.3 %collective-permute-start.4 = (bf16[256,512]{1,0:T(8,128)(2,1)S(1)}, bf16[256,512]{1,0:T(8,128)(2,1)S(1)}, u32[]{:S(2)}, u32[]{:S(2)}) collective-permute-start(bf16[256,512]{1,0:T(8,128)(2,1)S(1)} %convolution_convert_fusion.3), channel_id=1, source_target_pairs={{0,1},{1,0},{2,3},{3,2},{4,5},{5,4},{6,7},{7,6},{8,9},{9,8},{10,11... | collective-permute-start | bytes 786440 | tf_op jit(solution)/shard_map/ppermute | solution.py:41
  139.7 67.4 %collective-permute-start.15 = (bf16[1024,256]{1,0:T(8,128)(2,1)}, bf16[1024,256]{1,0:T(8,128)(2,1)}, u32[]{:S(2)}, u32[]{:S(2)}) collective-permute-start(bf16[1024,256]{1,0:T(8,128)(2,1)} %dynamic-slice_convert_fusion), channel_id=1, source_target_pairs={{0,16},{16,0},{1,17},{17,1},{2,18},{18,2},{3,19},{19,3},{4,20},{20... | collective-permute-start | bytes 1572872 | tf_op jit(solution)/shard_map/ppermute | solution.py:49
  140.6 68.6 %collective-permute-start.14 = (bf16[256,1024]{1,0:T(8,128)(2,1)}, bf16[256,1024]{1,0:T(8,128)(2,1)}, u32[]{:S(2)}, u32[]{:S(2)}) collective-permute-start(bf16[256,1024]{1,0:T(8,128)(2,1)} %dynamic-slice_convert_fusion.1), channel_id=1, source_target_pairs={{0,16},{16,0},{1,17},{17,1},{2,18},{18,2},{3,19},{19,3},{4,20},{20... | collective-permute-start | bytes 1572872 | tf_op jit(solution)/shard_map/ppermute | solution.py:49
  155.6 8.7 %collective-permute-start.5 = (bf16[256,512]{1,0:T(8,128)(2,1)S(1)}, bf16[256,512]{1,0:T(8,128)(2,1)S(1)}, u32[]{:S(2)}, u32[]{:S(2)}) collective-permute-start(bf16[256,512]{1,0:T(8,128)(2,1)S(1)} %copy-done.24), channel_id=1, source_target_pairs={{0,1},{1,0},{2,3},{3,2},{4,5},{5,4},{6,7},{7,6},{8,9},{9,8},{10,11... | collective-permute-start | bytes 786440 | tf_op jit(solution)/shard_map/ppermute | solution.py:41
  166.5 11.5 %all-to-all-start.3 = ((bf16[4,64,256]{2,1,0:T(8,128)(2,1)}), bf16[4,64,256]{2,1,0:T(8,128)(2,1)S(1)}, u32[]{:S(2)}, u32[]{:S(2)}) async-start(bf16[4,64,256]{2,1,0:T(8,128)(2,1)} %bitcast.36), calls=%async_computation.3 | async-start | bytes 262144 | tf_op jit(solution)/shard_map/all_to_all | solution.py:274
  192.0 7.4 %collective-permute-start.6 = (bf16[4,128,256]{2,1,0:T(8,128)(2,1)S(1)}, bf16[4,128,256]{2,1,0:T(8,128)(2,1)S(1)}, u32[]{:S(2)}, u32[]{:S(2)}) collective-permute-start(bf16[4,128,256]{2,1,0:T(8,128)(2,1)S(1)} %slice.298), channel_id=1, source_target_pairs={{0,2},{2,0},{4,6},{6,4},{8,10},{10,8},{12,14},{14,12},{1,3},{3,1},... | collective-permute-start | bytes 786440 | tf_op jit(solution)/shard_map/ppermute | solution.py:445
  195.9 27.5 %collective-permute-start.19 = (bf16[3,256]{1,0:T(4,128)(2,1)}, bf16[3,256]{1,0:T(4,128)(2,1)}, u32[]{:S(2)}, u32[]{:S(2)}) collective-permute-start(bf16[3,256]{1,0:T(4,128)(2,1)} %fusion.77), channel_id=1, source_target_pairs={{0,16},{16,0},{1,17},{17,1},{2,18},{18,2},{3,19},{19,3},{4,20},{20... | collective-permute-start | bytes 4616 | tf_op jit(solution)/shard_map/ppermute | solution.py:49
  195.9 28.2 %collective-permute-start.17 = (bf16[3,256]{1,0:T(4,128)(2,1)}, bf16[3,256]{1,0:T(4,128)(2,1)}, u32[]{:S(2)}, u32[]{:S(2)}) collective-permute-start(bf16[3,256]{1,0:T(4,128)(2,1)} %fusion.71), channel_id=1, source_target_pairs={{0,16},{16,0},{1,17},{17,1},{2,18},{18,2},{3,19},{19,3},{4,20},{20... | collective-permute-start | bytes 4616 | tf_op jit(solution)/shard_map/ppermute | solution.py:49
  199.4 25.4 %collective-permute-start.18 = (bf16[3,256]{1,0:T(4,128)(2,1)}, bf16[3,256]{1,0:T(4,128)(2,1)}, u32[]{:S(2)}, u32[]{:S(2)}) collective-permute-start(bf16[3,256]{1,0:T(4,128)(2,1)} %fusion.74), channel_id=1, source_target_pairs={{0,16},{16,0},{1,17},{17,1},{2,18},{18,2},{3,19},{19,3},{4,20},{20... | collective-permute-start | bytes 4616 | tf_op jit(solution)/shard_map/ppermute | solution.py:49
  202.3 16.8 %all-to-all-start.4 = ((bf16[4,192,256]{2,1,0:T(8,128)(2,1)}), bf16[4,192,256]{2,1,0:T(8,128)(2,1)}, u32[]{:S(2)}, u32[]{:S(2)}) async-start(bf16[4,192,256]{2,1,0:T(8,128)(2,1)} %pad_maximum_fusion.4), calls=%async_computation.4 | async-start | bytes 786432 | tf_op jit(solution)/shard_map/all_to_all | solution.py:274
  207.1 18.3 %collective-permute-start.10 = (bf16[256,256]{1,0:T(8,128)(2,1)}, bf16[256,256]{1,0:T(8,128)(2,1)S(1)}, u32[]{:S(2)}, u32[]{:S(2)}) collective-permute-start(bf16[256,256]{1,0:T(8,128)(2,1)} %dynamic-slice_convert_fusion.5), channel_id=1, source_target_pairs={{0,16},{16,0},{1,17},{17,1},{2,18},{18,2},{3,19},{19,3},{4,20},{20... | collective-permute-start | bytes 393224 | tf_op jit(solution)/shard_map/ppermute | solution.py:49
  219.1 30.1 %all-to-all-start.5 = ((bf16[8,128,512]{1,2,0:T(8,128)(2,1)}), bf16[8,128,512]{1,2,0:T(8,128)(2,1)}, u32[]{:S(2)}, u32[]{:S(2)}) async-start(bf16[8,128,512]{1,2,0:T(8,128)(2,1)} %pad_maximum_fusion.1), calls=%async_computation.5 | async-start | bytes 2097152 | tf_op jit(solution)/shard_map/all_to_all | solution.py:22
  229.0 24.0 %collective-permute-start.9 = (bf16[3,256,256]{1,2,0:T(8,128)(2,1)}, bf16[3,256,256]{1,2,0:T(8,128)(2,1)}, u32[]{:S(2)}, u32[]{:S(2)}) collective-permute-start(bf16[3,256,256]{1,2,0:T(8,128)(2,1)} %dynamic-slice_convert_fusion.2), channel_id=1, source_target_pairs={{0,16},{16,0},{1,17},{17,1},{2,18},{18,2},{3,19},{19,3},{4,20},{20... | collective-permute-start | bytes 1179656 | tf_op jit(solution)/shard_map/ppermute | solution.py:49
  344.1 54.4 %all-to-all-start.7 = ((bf16[8,272,512]{2,1,0:T(8,128)(2,1)}), bf16[8,272,512]{2,1,0:T(8,128)(2,1)S(1)}, u32[]{:S(2)}, u32[]{:S(2)}) async-start(bf16[8,272,512]{2,1,0:T(8,128)(2,1)} %broadcast_in_dim.34), calls=%async_computation.7 | async-start | bytes 4456448 | tf_op jit(solution)/shard_map/all_to_all | solution.py:54
  351.9 8.5 %collective-permute-start.7 = (bf16[256,512]{1,0:T(8,128)(2,1)S(1)}, bf16[256,512]{1,0:T(8,128)(2,1)S(1)}, u32[]{:S(2)}, u32[]{:S(2)}) collective-permute-start(bf16[256,512]{1,0:T(8,128)(2,1)S(1)} %fusion.16), channel_id=1, source_target_pairs={{0,1},{1,0},{2,3},{3,2},{4,5},{5,4},{6,7},{7,6},{8,9},{9,8},{10,11... | collective-permute-start | bytes 786440 | tf_op jit(solution)/shard_map/ppermute | solution.py:41
  353.8 7.9 %collective-permute-start.8 = (bf16[128,512]{1,0:T(8,128)(2,1)S(1)}, bf16[128,512]{1,0:T(8,128)(2,1)S(1)}, u32[]{:S(2)}, u32[]{:S(2)}) collective-permute-start(bf16[128,512]{1,0:T(8,128)(2,1)S(1)} %fusion.19), channel_id=1, source_target_pairs={{0,1},{1,0},{2,3},{3,2},{4,5},{5,4},{6,7},{7,6},{8,9},{9,8},{10,11... | collective-permute-start | bytes 393224 | tf_op jit(solution)/shard_map/ppermute | solution.py:41
  401.1 20.5 %collective-permute-start.20 = (f32[1032]{0:T(1024)S(1)}, f32[1032]{0:T(1024)S(1)}, u32[]{:S(2)}, u32[]{:S(2)}) collective-permute-start(f32[1032]{0:T(1024)S(1)} %slice_convert_fusion.2), channel_id=1, source_target_pairs={{0,16},{16,0},{1,17},{17,1},{2,18},{18,2},{3,19},{19,3},{4,20},{20... | collective-permute-start | bytes 12392 | tf_op jit(solution)/shard_map/ppermute | solution.py:512
  (69 other events, 674.8 us)
Sparse Core Ops, SparseCore 0:
  25.7 10.4 all-gather.3
  109.9 6.6 all-gather.5

commit v3 on v2

--- a/solution.py
+++ b/solution.py
@@ -41,12 +41,24 @@
     return part.astype(jnp.float32) + lax.ppermute(part, "tp", other("tp")).astype(jnp.float32)
 
 
-def pair_scatter(x, dim):
-    half = x.shape[dim] // 2
-    me = lax.axis_index("fsdp")
-    sent = lax.dynamic_slice_in_dim(x, (1 - me) * half, half, dim).astype(jnp.bfloat16)
-    kept = lax.dynamic_slice_in_dim(x, me * half, half, dim)
-    return kept + lax.ppermute(sent, "fsdp", other("fsdp")).astype(jnp.float32)
+def scattered(pairs, own_rows, other_rows, flipped=False):
+    half = pairs[0][1].shape[1] // 2
+    product = matmul if flipped else matmul_tn
+    sent = [product(a, b[:, half:]).astype(jnp.bfloat16) for a, b in pairs]
+    sent += [r.astype(jnp.bfloat16) for r in other_rows]
+    kept = [product(a, b[:, :half]) for a, b in pairs] + list(own_rows)
+    size = lax.axis_size("ctx")
+    total = sum(k.shape[0] for k in kept)
+    pad = -total % (16 * size)
+    arrived = lax.ppermute(jnp.concatenate(sent), "fsdp", other("fsdp"))
+    done, at = [], 0
+    for k in kept:
+        piece = arrived[at : at + k.shape[0]].astype(jnp.float32)
+        done.append((k + piece).astype(jnp.bfloat16))
+        at += k.shape[0]
+    if pad:
+        done.append(jnp.zeros((pad, half), jnp.bfloat16))
+    return jnp.concatenate(done)
 
 
 def gather_by_exchange(x, axis):
@@ -299,26 +311,32 @@
     norm_gain,
     norm_bias,
 ):
-    w_qkv, w_out, w_cq, w_ckv, w_co, w_in, w_fout, b_attn, b_out, gains, shifts = (
-        lax.all_gather(self_qkv, "fsdp", axis=1, tiled=True),
-        lax.all_gather(self_out, "fsdp", axis=1, tiled=True),
-        lax.all_gather(cross_q, "fsdp", axis=0, tiled=True),
-        lax.all_gather(cross_kv, "fsdp", axis=1, tiled=True),
-        lax.all_gather(cross_out, "fsdp", axis=1, tiled=True),
-        lax.all_gather(ffn_in, "fsdp", axis=0, tiled=True),
-        lax.all_gather(ffn_out, "fsdp", axis=1, tiled=True),
-        lax.all_gather(attn_bias.astype(jnp.bfloat16), "fsdp", axis=0, tiled=True).astype(
-            attn_bias.dtype
-        ),
-        lax.all_gather(out_bias.astype(jnp.bfloat16), "fsdp", axis=1, tiled=True).astype(
-            out_bias.dtype
-        ),
-        lax.all_gather(norm_gain.astype(jnp.bfloat16), "fsdp", axis=1, tiled=True).astype(
-            norm_gain.dtype
-        ),
-        lax.all_gather(norm_bias.astype(jnp.bfloat16), "fsdp", axis=1, tiled=True).astype(
-            norm_bias.dtype
-        ),
+    me = lax.axis_index("fsdp")
+    half = norm_gain.shape[1]
+
+    def swapped(x):
+        return jnp.where(me == 0, x, jnp.roll(x, half, axis=-1))
+
+    def with_other(x, dim):
+        return jnp.concatenate([x, lax.ppermute(x, "fsdp", other("fsdp"))], axis=dim)
+
+    w_qkv = with_other(self_qkv, 1)
+    small = jnp.concatenate([attn_bias, out_bias, norm_gain, norm_bias])
+    small_other = lax.ppermute(small, "fsdp", other("fsdp"))
+    small_both = jnp.concatenate([small, small_other], axis=1)
+    b_attn = jnp.where(
+        me == 0,
+        jnp.concatenate([attn_bias, small_other[:2]]),
+        jnp.concatenate([small_other[:2], attn_bias]),
+    )
+    b_out, gains, shifts = small_both[2:5], small_both[5:8], small_both[8:11]
+    w_out, w_cq, w_ckv, w_co, w_in, w_fout = (
+        with_other(self_out, 1),
+        with_other(cross_q, 0),
+        with_other(cross_kv, 1),
+        with_other(cross_out, 1),
+        with_other(ffn_in, 0),
+        with_other(ffn_out, 1),
     )
 
     def head_total(partial_value):
@@ -328,7 +346,8 @@
         stacked = gather_by_exchange(x, "ctx")
         return stacked.reshape((-1,) + x.shape[1:])
 
-    inputs = tokens[0]
+    inputs = swapped(tokens[0])
+    states_own = swapped(source_states[0])
     resid_in = inputs.astype(jnp.float32)
     query_segs = block_ids[0]
     rows = inputs.shape[0]
@@ -338,6 +357,7 @@
     packed = (packed + shift_v[:, :, None]).astype(jnp.bfloat16)
     packed = packed.reshape(3, local_heads, HEAD, rows).swapaxes(0, 1)
     packed = packed.reshape(local_heads, 3 * HEAD, rows)
+    states_all = over_ctx(states_own)
     seg_rows = jnp.broadcast_to(query_segs.astype(jnp.bfloat16), (local_heads, 16, rows))
     own = to_heads(jnp.concatenate([packed, seg_rows], axis=1))
     members = lax.axis_size("ctx") // local_heads
@@ -349,12 +369,12 @@
     low = kv[:, 2 * HEAD, 0].astype(jnp.int32)
     high = kv[:local_heads, 2 * HEAD, rows - 1].astype(jnp.int32)
     head_out, log_sum = attend(low, high, own, kv)
+    head_out, states_all = lax.optimization_barrier((head_out, states_all))
     mixed_t = to_heads(head_out.astype(jnp.bfloat16)).reshape(-1, rows)
     mixed_low = mixed_t.T
     self_branch = head_total(matmul(mixed_low, w_out)) + b_out[0]
     first, first_norm, first_inv = norm_forward(resid_in + self_branch, gains[0], shifts[0])
     first_low = first.astype(jnp.bfloat16)
-    states_all = over_ctx(source_states[0])
     cross_query = (matmul(first_low, w_cq) + b_attn[2]).astype(jnp.bfloat16)
     cross_keys = matmul(states_all, w_ckv[0]).astype(jnp.bfloat16)
     cross_values = (matmul(states_all, w_ckv[1]) + b_attn[3]).astype(jnp.bfloat16)
@@ -384,15 +404,16 @@
     ffn_branch = head_total(matmul(active, w_fout)) + b_out[2]
     result, third_norm, third_inv = norm_forward(second + ffn_branch, gains[2], shifts[2])
     grad_third, gain_third, shift_third = norm_backward(
-        out_grad[0].astype(jnp.float32), third_norm, third_inv, gains[2]
+        swapped(out_grad[0]).astype(jnp.float32), third_norm, third_inv, gains[2]
     )
     grad_ffn_low = grad_third.astype(jnp.bfloat16)
     grad_active = matmul_nt(grad_ffn_low, w_fout)
     grad_hidden = (grad_active * sigma * (1.0 + hidden * (1.0 - sigma))).astype(jnp.bfloat16)
     grad_second_in = grad_third + head_total(matmul_nt(grad_hidden, w_in))
-    g_fin = matmul_tn(second_low, grad_hidden)
     g_fbias = jnp.sum(grad_hidden.astype(jnp.float32), axis=0)
-    g_fout = matmul_tn(active, grad_ffn_low)
+    ffn_sum = ctx_total(
+        scattered(((grad_hidden, second_low), (active, grad_ffn_low)), (), ())
+    )
     grad_second, gain_second, shift_second = norm_backward(
         grad_second_in, second_norm, second_inv, gains[1]
     )
@@ -426,16 +447,25 @@
     )
     grad_ck_low = grad_ck.astype(jnp.bfloat16)
     grad_cv_low = grad_cv.astype(jnp.bfloat16)
-    local_states = source_states[0]
-    g_ckv = jnp.stack([matmul_tn(local_states, grad_ck_low), matmul_tn(local_states, grad_cv_low)])
     source_part = matmul_nt(grad_ck_low, w_ckv[0]) + matmul_nt(grad_cv_low, w_ckv[1])
     grad_first_in = grad_second + head_total(matmul_nt(grad_cq, w_cq))
-    g_cq = matmul_tn(first_low, grad_cq)
-    g_co = matmul_tn(looked, grad_cross_low)
     grad_first, gain_first, shift_first = norm_backward(
         grad_first_in, first_norm, first_inv, gains[0]
     )
     grad_self_low = grad_first.astype(jnp.bfloat16)
+    middle_sum = ctx_total(
+        scattered(
+            (
+                (mixed_low, grad_self_low),
+                (grad_cq, first_low),
+                (grad_ck_low, states_own),
+                (grad_cv_low, states_own),
+                (looked, grad_cross_low),
+            ),
+            (),
+            (),
+        )
+    )
     grad_mixed = matmul_nt(grad_self_low, w_out).astype(jnp.bfloat16)
     grads_in = to_heads(grad_mixed.T.reshape(local_heads, HEAD, rows))
     part_q, part_kv = attend_back(low, high, own, kv, grads_in, head_out, log_sum)
@@ -454,36 +484,6 @@
         tp_total(source_part.astype(jnp.bfloat16)),
     )
     input_grad = grad_first + input_sum
-    g_qkv = jnp.stack(
-        [matmul_tn(inputs, grad_q), matmul_tn(inputs, grad_k), matmul_tn(inputs, grad_v)]
-    )
-    g_out = matmul_tn(mixed_low, grad_self_low)
-    g_abias = jnp.stack(
-        [
-            jnp.sum(grad_q.astype(jnp.float32), axis=0),
-            jnp.sum(grad_v.astype(jnp.float32), axis=0),
-            jnp.sum(grad_cq.astype(jnp.float32), axis=0),
-            jnp.sum(grad_cv_low.astype(jnp.float32), axis=0),
-        ]
-    )
-    g_obias = jnp.stack(
-        [jnp.sum(grad_first, axis=0), jnp.sum(grad_second, axis=0), jnp.sum(grad_third, axis=0)]
-    )
-    g_gain = jnp.stack([gain_first, gain_second, gain_third])
-    g_shift = jnp.stack([shift_first, shift_second, shift_third])
-    big = (
-        (g_qkv, 1),
-        (g_out, 1),
-        (g_cq, 0),
-        (g_ckv, 1),
-        (g_co, 1),
-        (g_fin, 0),
-        (g_fout, 1),
-        (g_abias, 0),
-        (g_obias, 1),
-        (g_gain, 1),
-        (g_shift, 1),
-    )
     squares = jnp.stack(
         [
             jnp.sum(resid_in * resid_in),
@@ -492,32 +492,61 @@
             jnp.sum(ffn_branch * ffn_branch),
         ]
     )
-    square_high = squares.astype(jnp.bfloat16)
-    square_low = (squares - square_high.astype(jnp.float32)).astype(jnp.bfloat16)
-    extra = jnp.concatenate([g_fbias.astype(jnp.bfloat16), square_high, square_low])
-    halves = [pair_scatter(g, dim) for g, dim in big]
-    flats = [h.astype(jnp.bfloat16).reshape(-1) for h in halves]
-    size = lax.axis_size("ctx")
-    flats.append(extra)
-    lengths = [f.shape[0] for f in flats]
-    pad = -sum(lengths) % (512 * 16 * size)
-    packed = jnp.concatenate(flats + [jnp.zeros((pad,), jnp.bfloat16)]).reshape(-1, 512)
-    summed = ctx_total(packed).reshape(-1).astype(jnp.float32)
-    outs, at = [], 0
-    for h, length in zip(halves, lengths):
-        outs.append(summed[at : at + length].reshape(h.shape))
-        at += length
-    o_qkv, o_out, o_cq, o_ckv, o_co, o_fin, o_fout, o_abias, o_obias, o_gain, o_shift = outs
-    extra_sum = summed[at : at + lengths[-1]]
-    extra_sum = extra_sum + lax.ppermute(extra_sum, "fsdp", other("fsdp"))
-    fbias_total = extra_sum[:-8]
-    square_total = extra_sum[-8:-4] + extra_sum[-4:]
+    square_high = squares.astype(jnp.bfloat16).astype(jnp.float32)
+    square_row = jnp.concatenate(
+        [square_high, squares - square_high, jnp.zeros((half - 8,), jnp.float32)]
+    )[None]
+    feature_rows = jnp.stack(
+        [
+            jnp.sum(grad_first, axis=0),
+            jnp.sum(grad_second, axis=0),
+            jnp.sum(grad_third, axis=0),
+            gain_first,
+            gain_second,
+            gain_third,
+            shift_first,
+            shift_second,
+            shift_third,
+        ]
+    )
+    self_rows = jnp.stack(
+        [jnp.sum(grad_q.astype(jnp.float32), axis=0), jnp.sum(grad_v.astype(jnp.float32), axis=0)]
+    )
+    cross_rows = jnp.stack(
+        [
+            jnp.sum(grad_cq.astype(jnp.float32), axis=0),
+            jnp.sum(grad_cv_low.astype(jnp.float32), axis=0),
+        ]
+    )
+    common = jnp.concatenate([g_fbias.reshape(-1, half), square_row])
+    tail = scattered(
+        ((back.reshape(-1, rows), inputs),),
+        (feature_rows[:, :half], jnp.where(me == 0, self_rows, cross_rows), common),
+        (feature_rows[:, half:], jnp.where(me == 0, cross_rows, self_rows), common),
+        flipped=True,
+    )
+    tail_sum = ctx_total(tail).astype(jnp.float32)
+    width = w_qkv.shape[2]
+    o_qkv = tail_sum[: 3 * width].reshape(3, width, half).swapaxes(1, 2)
+    at = 3 * width
+    o_obias, o_gain, o_shift = (tail_sum[at + 3 * i : at + 3 * i + 3] for i in range(3))
+    o_abias = tail_sum[at + 9 : at + 11]
+    hidden_rows = g_fbias.shape[0] // half
+    fbias_total = tail_sum[at + 11 : at + 11 + hidden_rows].reshape(-1)
+    square_sums = tail_sum[at + 11 + hidden_rows]
+    square_total = square_sums[:4] + square_sums[4:8]
+    middle_sum, ffn_sum = middle_sum.astype(jnp.float32), ffn_sum.astype(jnp.float32)
+    o_out, o_cq, o_ck, o_cv, o_co = (middle_sum[i * width : (i + 1) * width] for i in range(5))
+    o_cq = o_cq.T
+    o_ckv = jnp.stack([o_ck.T, o_cv.T])
+    hidden_width = g_fbias.shape[0]
+    o_fin, o_fout = ffn_sum[:hidden_width].T, ffn_sum[hidden_width : 2 * hidden_width]
     entries = rows * inputs.shape[1] * lax.axis_size("fsdp") * lax.axis_size("ctx")
     rms_values = jnp.sqrt(square_total / entries)
     return (
-        result[None].astype(jnp.bfloat16),
-        input_grad[None],
-        source_sum[None],
+        swapped(result.astype(jnp.bfloat16))[None],
+        swapped(input_grad)[None],
+        swapped(source_sum)[None],
         rms_values,
         o_qkv,
         o_out,

time: 435 us -> 364 us (0.84)
  blocking collectives: 73.5 us -> 0 us
  local copies, waits for them, and re-layouts: 75.6 us -> 39.6 us
  matrix products: 32.5 us -> 54.6 us
  starting transfers between devices: 48.8 us -> 69.5 us
  between operations: 15.7 us -> 2.38 us
  other arithmetic: 44.1 us -> 51.4 us
    all_to_all x1 -> x0, blocking collectives: 55.4 us -> none  [ctx_total(): lax.all_to_all(pieces, 'ctx', split_axis=0, concat_axis=0, tiled=True)]
    all_to_all x0 -> x3, waiting for transfers between devices: none -> 27.4 us  [ctx_total(): lax.all_to_all(pieces, 'ctx', split_axis=0, concat_axis=0, tiled=True)]
    dot_general x10 -> x14, matrix products: 3.8 us -> 23.3 us  [matmul_tn(): lax.dot_general(left, right, (((0,), (0,)), ((), ())), preferred_element_...]
    concatenate x1 -> x7, local copies, waits for them, and re-layouts: 24.8 us -> 6.1 us  [the longest x1 3.89 us: scattered(): return jnp.concatenate(done)]
    all_gather x9 -> x0, blocking collectives: 18.1 us -> none  [the longest x1 2.37 us: per_device(): lax.all_gather(self_qkv, 'fsdp', axis=1, tiled=True)]
    all_to_all x2 -> x4, waiting for transfers between devices: 49.3 us -> 33.2 us  [gather_by_exchange(): lax.all_to_all(jnp.broadcast_to(x[None], (size,) + x.shape), axis, split_...]
    convert_element_type x16 -> x0, local copies, waits for them, and re-layouts: 16 us -> none  [the longest x3 7.51 us: per_device(): summed = ctx_total(packed).reshape(-1).astype(jnp.float32)]
    all_to_all x0 -> x3, starting transfers between devices: none -> 10.7 us  [ctx_total(): lax.all_to_all(pieces, 'ctx', split_axis=0, concat_axis=0, tiled=True)]
  transfers between devices with their start and end apart: 30 -> 32, of which waited for: 15 -> 19; matrix products, arithmetic and copies ran while one was open for 23% -> 32% of each run, Pallas kernels for 6% -> 3%
where the time goes in v3:
time: 364 us; the launch traced here: 361 us
  waiting for transfers between devices  119 us (33%)
  starting transfers between devices  69.5 us (19%)
  matrix products  54.6 us (15%)
  other arithmetic  51.4 us (14%)
  local copies, waits for them, and re-layouts  39.6 us (11%)
  Pallas kernels  24.4 us (7%)
    all_to_all x4, waiting for transfers between devices, gather_by_exchange(): lax.all_to_all(jnp.broadcast_to(x[None], (size,) + x.shape), axis, split_...  33.2 us
    all_to_all x3, waiting for transfers between devices, ctx_total(): lax.all_to_all(pieces, 'ctx', split_axis=0, concat_axis=0, tiled=True)  27.4 us
    dot_general x14, matrix products, matmul_tn(): lax.dot_general(left, right, (((0,), (0,)), ((), ())), preferred_element_...  23.3 us
    all_to_all x4, waiting for transfers between devices, to_heads(): lax.all_to_all(pieces, 'ctx', 0, 0, axis_index_groups=groups, tiled=True)  20.6 us
    all_to_all x4, starting transfers between devices, to_heads(): lax.all_to_all(pieces, 'ctx', 0, 0, axis_index_groups=groups, tiled=True)  19.5 us
    ppermute x7, waiting for transfers between devices, tp_total(): lax.ppermute(part, 'tp', other('tp')).astype(jnp.float32)  16.5 us
    all_to_all x4, starting transfers between devices, gather_by_exchange(): lax.all_to_all(jnp.broadcast_to(x[None], (size,) + x.shape), axis, split_...  15.6 us
    unnamed x141, local copies, waits for them, and re-layouts  12.8 us
  transfers between devices with their start and end apart: 32, of which 19 were waited for; matrix products, arithmetic and copies ran while one was open for 32% of the time, Pallas kernels for 3%

profile of v3, /device:TPU:0, one launch (start us, length us, event | category | flops | bytes accessed | tf_op | source)
XLA Modules:
  0.0 360.8 jit_solution(9607250755976309386)
XLA Ops:
  9.4 6.3 %all-to-all-start = ((bf16[4,208,256]{2,1,0:T(8,128)(2,1)}), bf16[4,208,256]{2,1,0:T(8,128)(2,1)S(1)}, u32[]{:S(2)}, u32[]{:S(2)}) async-start(bf16[4,208,256]{2,1,0:T(8,128)(2,1)} %pad_maximum_fusion.7), calls=%async_computation | async-start | bytes 851968 | tf_op jit(solution)/shard_map/all_to_all | solution.py:286
  16.5 11.9 %all-to-all-done.q_ref = bf16[4,208,256]{2,1,0:T(8,128)(2,1)S(1)} async-done(((bf16[4,208,256]{2,1,0:T(8,128)(2,1)}), bf16[4,208,256]{2,1,0:T(8,128)(2,1)S(1)}, u32[]{:S(2)}, u32[]{:S(2)}) %all-to-all-start) | async-done | bytes 426016 | tf_op jit(solution)/shard_map/all_to_all | solution.py:286
  29.5 3.7 %all-to-all-start.1 = ((bf16[8,128,512]{2,1,0:T(8,128)(2,1)}), bf16[8,128,512]{2,1,0:T(8,128)(2,1)S(1)}, u32[]{:S(2)}, u32[]{:S(2)}) async-start(bf16[8,128,512]{2,1,0:T(8,128)(2,1)} %broadcast_in_dim.38), calls=%async_computation.1 | async-start | bytes 2097152 | tf_op jit(solution)/shard_map/all_to_all | solution.py:66
  47.9 8.7 %collective-permute-done.2 = bf16[4,144,256]{2,1,0:T(8,128)(2,1)S(1)} collective-permute-done((bf16[4,144,256]{2,1,0:T(8,128)(2,1)S(1)}, bf16[4,144,256]{2,1,0:T(8,128)(2,1)S(1)}, u32[]{:S(2)}, u32[]{:S(2)}) %collective-permute-start.2) | collective-permute-done | bytes 294944 | tf_op jit(solution)/shard_map/ppermute | solution.py:367
  58.2 12.0 %attend.1 = (f32[4,64,256]{2,1,0:T(8,128)}, f32[4,1,256]{2,1,0:T(1,128)}) custom-call(s32[8]{0:T(128)} %convert_reduce_fusion.6.low_ref, s32[4]{0:T(128)} %fusion.113.high_ref, bf16[4,208,256]{2,1,0:T(8,128)(2,1)} %copy-done.23, bf16[8,144,256]{2,1,0:T(8,128)(2,1)} %pad_maximum_fusion.5.kv_ref), custom_call_target="tpu_custom_call" | custom-call | flops 268435456 | bytes 589824 | tf_op jit(solution)/shard_map/attend/pallas_call | solution.py:224
  71.9 4.8 %all-to-all-start.2 = ((bf16[4,64,256]{2,1,0:T(8,128)(2,1)}), bf16[4,64,256]{2,1,0:T(8,128)(2,1)}, u32[]{:S(2)}, u32[]{:S(2)}) async-start(bf16[4,64,256]{2,1,0:T(8,128)(2,1)} %convert_element_type.341), calls=%async_computation.2 | async-start | bytes 262144 | tf_op jit(solution)/shard_map/all_to_all | solution.py:286
  79.0 3.9 %all-to-all-done.2 = bf16[4,64,256]{2,1,0:T(8,128)(2,1)} async-done(((bf16[4,64,256]{2,1,0:T(8,128)(2,1)}), bf16[4,64,256]{2,1,0:T(8,128)(2,1)}, u32[]{:S(2)}, u32[]{:S(2)}) %all-to-all-start.2) | async-done | bytes 131104 | tf_op jit(solution)/shard_map/all_to_all | solution.py:286
  94.2 4.6 %fusion.143 = (f32[256,4]{0,1:T(4,128)S(1)}, f32[256,4,1024]{0,2,1:T(8,128)}) fusion(pred[1024]{0:T(1024)(128)(4,1)} %iota_compare_fusion, bf16[1024,4,64]{0,2,1:T(8,128)(2,1)} %bitcast.215, bf16[256,4,64]{0,2,1:T(8,128)(2,1)S(1)} %bitcast.238), kind=kOutput, calls=%fused_computation.291 | convolution fusion | flops 138413056 | bytes 4854784 | tf_op jit(solution)/shard_map/sub | solution.py:390
  112.4 4.9 %collective-permute-done.11 = bf16[256,512]{1,0:T(8,128)(2,1)S(1)} collective-permute-done((bf16[256,512]{1,0:T(8,128)(2,1)S(1)}, bf16[256,512]{1,0:T(8,128)(2,1)S(1)}, u32[]{:S(2)}, u32[]{:S(2)}) %collective-permute-start.11) | collective-permute-done | bytes 262176 | tf_op jit(solution)/shard_map/ppermute | solution.py:41
  144.0 4.2 %all-to-all-start.3 = ((bf16[4,64,256]{2,1,0:T(8,128)(2,1)}), bf16[4,64,256]{2,1,0:T(8,128)(2,1)S(1)}, u32[]{:S(2)}, u32[]{:S(2)}) async-start(bf16[4,64,256]{2,1,0:T(8,128)(2,1)} %bitcast.37), calls=%async_computation.3 | async-start | bytes 262144 | tf_op jit(solution)/shard_map/all_to_all | solution.py:286
  150.4 3.7 %all-to-all-done.3.g_ref = bf16[4,64,256]{2,1,0:T(8,128)(2,1)S(1)} async-done(((bf16[4,64,256]{2,1,0:T(8,128)(2,1)}), bf16[4,64,256]{2,1,0:T(8,128)(2,1)S(1)}, u32[]{:S(2)}, u32[]{:S(2)}) %all-to-all-start.3) | async-done | bytes 131104 | tf_op jit(solution)/shard_map/all_to_all | solution.py:286
  154.7 12.4 %attend_back.1 = (bf16[4,64,256]{2,1,0:T(8,128)(2,1)}, f32[8,128,256]{2,1,0:T(8,128)}) custom-call(s32[8]{0:T(128)} %convert_reduce_fusion.6.low_ref, s32[4]{0:T(128)} %fusion.113.high_ref, bf16[4,208,256]{2,1,0:T(8,128)(2,1)} %copy-done.23, bf16[8,144,256]{2,1,0:T(8,128)(2,1)} %pad_maximum_fusion.5.kv_ref, bf16[4,64,256]{2,1,0:T(8,128)(2,1)} %copy-done.42, ...), custom_call_target="tpu_custom_call" | custom-call | flops 671088640 | bytes 2359296 | tf_op jit(solution)/shard_map/attend_back/pallas_call | solution.py:252
  178.2 4.1 %all-to-all-start.4 = ((bf16[4,192,256]{2,1,0:T(8,128)(2,1)}), bf16[4,192,256]{2,1,0:T(8,128)(2,1)}, u32[]{:S(2)}, u32[]{:S(2)}) async-start(bf16[4,192,256]{2,1,0:T(8,128)(2,1)} %pad_maximum_fusion.9), calls=%async_computation.4 | async-start | bytes 786432 | tf_op jit(solution)/shard_map/all_to_all | solution.py:286
  191.8 5.4 %all-to-all-start.5 = ((bf16[8,128,512]{1,2,0:T(8,128)(2,1)}), bf16[8,128,512]{1,2,0:T(8,128)(2,1)S(1)}, u32[]{:S(2)}, u32[]{:S(2)}) async-start(bf16[8,128,512]{1,2,0:T(8,128)(2,1)} %pad_maximum_fusion.1), calls=%async_computation.5 | async-start | bytes 2097152 | tf_op jit(solution)/shard_map/all_to_all | solution.py:22
  209.8 9.3 %all-to-all-done.5 = bf16[8,128,512]{1,2,0:T(8,128)(2,1)S(1)} async-done(((bf16[8,128,512]{1,2,0:T(8,128)(2,1)}), bf16[8,128,512]{1,2,0:T(8,128)(2,1)S(1)}, u32[]{:S(2)}, u32[]{:S(2)}) %all-to-all-start.5) | async-done | bytes 1048608 | tf_op jit(solution)/shard_map/all_to_all | solution.py:22
  233.7 3.9 %concatenate.125 = bf16[896,256]{1,0:T(8,128)(2,1)} concatenate(bf16[768,256]{1,0:T(8,128)(2,1)S(1)} %add_convert_fusion.2, bf16[9,256]{1,0:T(8,128)(2,1)S(1)} %fusion.108, bf16[2,256]{1,0:T(2,128)(2,1)S(1)} %add_convert_fusion.10, bf16[5,256]{1,0:T(8,128)(2,1)S(1)} %fusion.111, bf16[112,256]{1,0:T(8,128)(2,1)S(1)} %broadcast_in_dim.46), dimensions={0} | concatenate | bytes 917504 | tf_op jit(solution)/shard_map/concatenate | solution.py:61
  239.5 7.7 %all-to-all-done.10 = bf16[8,256,256]{2,1,0:T(8,128)(2,1)S(1)} async-done(((bf16[8,256,256]{2,1,0:T(8,128)(2,1)}), bf16[8,256,256]{2,1,0:T(8,128)(2,1)S(1)}, u32[]{:S(2)}, u32[]{:S(2)}) %all-to-all-start.10) | async-done | bytes 1048608 | tf_op jit(solution)/shard_map/all_to_all | solution.py:74
  258.0 5.9 %all-to-all-done.6 = bf16[8,112,256]{2,1,0:T(8,128)(2,1)S(1)} async-done(((bf16[8,112,256]{2,1,0:T(8,128)(2,1)}), bf16[8,112,256]{2,1,0:T(8,128)(2,1)S(1)}, u32[]{:S(2)}, u32[]{:S(2)}) %all-to-all-start.6) | async-done | bytes 458784 | tf_op jit(solution)/shard_map/all_to_all | solution.py:74
  272.0 13.8 %all-to-all-done.8 = bf16[8,160,256]{2,1,0:T(8,128)(2,1)S(1)} async-done(((bf16[8,160,256]{2,1,0:T(8,128)(2,1)}), bf16[8,160,256]{2,1,0:T(8,128)(2,1)S(1)}, u32[]{:S(2)}, u32[]{:S(2)}) %all-to-all-start.8) | async-done | bytes 655392 | tf_op jit(solution)/shard_map/all_to_all | solution.py:74
  287.4 4.1 %all-to-all-start.7 = ((bf16[8,112,256]{2,1,0:T(8,128)(2,1)}), bf16[8,112,256]{2,1,0:T(8,128)(2,1)}, u32[]{:S(2)}, u32[]{:S(2)}) async-start(bf16[8,112,256]{2,1,0:T(8,128)(2,1)} %broadcast_in_dim.47), calls=%async_computation.7 | async-start | bytes 917504 | tf_op jit(solution)/shard_map/all_to_all | solution.py:66
  296.3 8.2 %all-to-all-done.7 = bf16[8,112,256]{2,1,0:T(8,128)(2,1)} async-done(((bf16[8,112,256]{2,1,0:T(8,128)(2,1)}), bf16[8,112,256]{2,1,0:T(8,128)(2,1)}, u32[]{:S(2)}, u32[]{:S(2)}) %all-to-all-start.7) | async-done | bytes 458784 | tf_op jit(solution)/shard_map/all_to_all | solution.py:66
  317.6 17.2 %all-to-all-done.11 = bf16[8,256,256]{2,1,0:T(8,128)(2,1)S(1)} async-done(((bf16[8,256,256]{2,1,0:T(8,128)(2,1)}), bf16[8,256,256]{2,1,0:T(8,128)(2,1)S(1)}, u32[]{:S(2)}, u32[]{:S(2)}) %all-to-all-start.11) | async-done | bytes 1048608 | tf_op jit(solution)/shard_map/all_to_all | solution.py:66
  335.7 4.2 %all-to-all-start.9 = ((bf16[8,160,256]{2,1,0:T(8,128)(2,1)}), bf16[8,160,256]{2,1,0:T(8,128)(2,1)}, u32[]{:S(2)}, u32[]{:S(2)}) async-start(bf16[8,160,256]{2,1,0:T(8,128)(2,1)} %broadcast_in_dim.48), calls=%async_computation.9 | async-start | bytes 1310720 | tf_op jit(solution)/shard_map/all_to_all | solution.py:66
  349.1 7.8 %all-to-all-done.9 = bf16[8,160,256]{2,1,0:T(8,128)(2,1)} async-done(((bf16[8,160,256]{2,1,0:T(8,128)(2,1)}), bf16[8,160,256]{2,1,0:T(8,128)(2,1)}, u32[]{:S(2)}, u32[]{:S(2)}) %all-to-all-start.9) | async-done | bytes 655392 | tf_op jit(solution)/shard_map/all_to_all | solution.py:66
  (339 shorter events, 185.6 us)
Async XLA Ops:
  9.4 18.9 %all-to-all-start = ((bf16[4,208,256]{2,1,0:T(8,128)(2,1)}), bf16[4,208,256]{2,1,0:T(8,128)(2,1)S(1)}, u32[]{:S(2)}, u32[]{:S(2)}) async-start(bf16[4,208,256]{2,1,0:T(8,128)(2,1)} %pad_maximum_fusion.7), calls=%async_computation | async-start | bytes 851968 | tf_op jit(solution)/shard_map/all_to_all | solution.py:286
  29.5 40.8 %all-to-all-start.1 = ((bf16[8,128,512]{2,1,0:T(8,128)(2,1)}), bf16[8,128,512]{2,1,0:T(8,128)(2,1)S(1)}, u32[]{:S(2)}, u32[]{:S(2)}) async-start(bf16[8,128,512]{2,1,0:T(8,128)(2,1)} %broadcast_in_dim.38), calls=%async_computation.1 | async-start | bytes 2097152 | tf_op jit(solution)/shard_map/all_to_all | solution.py:66
  33.2 13.9 %collective-permute-start.5 = (bf16[2,256,256]{2,1,0:T(8,128)(2,1)}, bf16[2,256,256]{2,1,0:T(8,128)(2,1)S(1)}, u32[]{:S(2)}, u32[]{:S(2)}) collective-permute-start(bf16[2,256,256]{2,1,0:T(8,128)(2,1)} %param.25), channel_id=1, source_target_pairs={{0,16},{16,0},{1,17},{17,1},{2,18},{18,2},{3,19},{19,3},{4,20},{20... | collective-permute-start | bytes 786440 | tf_op jit(solution)/shard_map/ppermute | solution.py:321
  33.2 11.1 %collective-permute-start.3 = (bf16[256,256]{1,0:T(8,128)(2,1)}, bf16[256,256]{1,0:T(8,128)(2,1)S(1)}, u32[]{:S(2)}, u32[]{:S(2)}) collective-permute-start(bf16[256,256]{1,0:T(8,128)(2,1)} %param.23), channel_id=1, source_target_pairs={{0,16},{16,0},{1,17},{17,1},{2,18},{18,2},{3,19},{19,3},{4,20},{20... | collective-permute-start | bytes 393224 | tf_op jit(solution)/shard_map/ppermute | solution.py:321
  33.7 11.2 %collective-permute-start.6 = (bf16[256,256]{1,0:T(8,128)(2,1)}, bf16[256,256]{1,0:T(8,128)(2,1)S(1)}, u32[]{:S(2)}, u32[]{:S(2)}) collective-permute-start(bf16[256,256]{1,0:T(8,128)(2,1)} %param.24), channel_id=1, source_target_pairs={{0,16},{16,0},{1,17},{17,1},{2,18},{18,2},{3,19},{19,3},{4,20},{20... | collective-permute-start | bytes 393224 | tf_op jit(solution)/shard_map/ppermute | solution.py:321
  33.8 13.2 %collective-permute-start.7 = (bf16[256,256]{1,0:T(8,128)(2,1)}, bf16[256,256]{1,0:T(8,128)(2,1)S(1)}, u32[]{:S(2)}, u32[]{:S(2)}) collective-permute-start(bf16[256,256]{1,0:T(8,128)(2,1)} %param.26), channel_id=1, source_target_pairs={{0,16},{16,0},{1,17},{17,1},{2,18},{18,2},{3,19},{19,3},{4,20},{20... | collective-permute-start | bytes 393224 | tf_op jit(solution)/shard_map/ppermute | solution.py:321
  34.3 69.4 %collective-permute-start.9 = (bf16[256,1024]{1,0:T(8,128)(2,1)}, bf16[256,1024]{1,0:T(8,128)(2,1)}, u32[]{:S(2)}, u32[]{:S(2)}) collective-permute-start(bf16[256,1024]{1,0:T(8,128)(2,1)} %param.27), channel_id=1, source_target_pairs={{0,16},{16,0},{1,17},{17,1},{2,18},{18,2},{3,19},{19,3},{4,20},{20... | collective-permute-start | bytes 1572872 | tf_op jit(solution)/shard_map/ppermute | solution.py:321
  44.4 60.4 %collective-permute-start.10 = (bf16[1024,256]{1,0:T(8,128)(2,1)}, bf16[1024,256]{1,0:T(8,128)(2,1)}, u32[]{:S(2)}, u32[]{:S(2)}) collective-permute-start(bf16[1024,256]{1,0:T(8,128)(2,1)} %param.28), channel_id=1, source_target_pairs={{0,16},{16,0},{1,17},{17,1},{2,18},{18,2},{3,19},{19,3},{4,20},{20... | collective-permute-start | bytes 1572872 | tf_op jit(solution)/shard_map/ppermute | solution.py:321
  45.0 11.6 %collective-permute-start.2 = (bf16[4,144,256]{2,1,0:T(8,128)(2,1)S(1)}, bf16[4,144,256]{2,1,0:T(8,128)(2,1)S(1)}, u32[]{:S(2)}, u32[]{:S(2)}) collective-permute-start(bf16[4,144,256]{2,1,0:T(8,128)(2,1)S(1)} %slice.386), channel_id=1, source_target_pairs={{0,2},{2,0},{4,6},{6,4},{8,10},{10,8},{12,14},{14,12},{1,3},{3,1},... | collective-permute-start | bytes 884744 | tf_op jit(solution)/shard_map/ppermute | solution.py:367
  71.9 11.0 %all-to-all-start.2 = ((bf16[4,64,256]{2,1,0:T(8,128)(2,1)}), bf16[4,64,256]{2,1,0:T(8,128)(2,1)}, u32[]{:S(2)}, u32[]{:S(2)}) async-start(bf16[4,64,256]{2,1,0:T(8,128)(2,1)} %convert_element_type.341), calls=%async_computation.2 | async-start | bytes 262144 | tf_op jit(solution)/shard_map/all_to_all | solution.py:286
  84.3 6.7 %collective-permute-start.4 = (bf16[256,512]{1,0:T(8,128)(2,1)S(1)}, bf16[256,512]{1,0:T(8,128)(2,1)S(1)}, u32[]{:S(2)}, u32[]{:S(2)}) collective-permute-start(bf16[256,512]{1,0:T(8,128)(2,1)S(1)} %convolution_convert_fusion.9), channel_id=1, source_target_pairs={{0,1},{1,0},{2,3},{3,2},{4,5},{5,4},{6,7},{7,6},{8,9},{9,8},{10,11... | collective-permute-start | bytes 786440 | tf_op jit(solution)/shard_map/ppermute | solution.py:41
  144.0 10.1 %all-to-all-start.3 = ((bf16[4,64,256]{2,1,0:T(8,128)(2,1)}), bf16[4,64,256]{2,1,0:T(8,128)(2,1)S(1)}, u32[]{:S(2)}, u32[]{:S(2)}) async-start(bf16[4,64,256]{2,1,0:T(8,128)(2,1)} %bitcast.37), calls=%async_computation.3 | async-start | bytes 262144 | tf_op jit(solution)/shard_map/all_to_all | solution.py:286
  168.2 7.1 %collective-permute-start.14 = (bf16[4,128,256]{2,1,0:T(8,128)(2,1)S(1)}, bf16[4,128,256]{2,1,0:T(8,128)(2,1)}, u32[]{:S(2)}, u32[]{:S(2)}) collective-permute-start(bf16[4,128,256]{2,1,0:T(8,128)(2,1)S(1)} %slice.599), channel_id=1, source_target_pairs={{0,2},{2,0},{4,6},{6,4},{8,10},{10,8},{12,14},{14,12},{1,3},{3,1},... | collective-permute-start | bytes 786440 | tf_op jit(solution)/shard_map/ppermute | solution.py:475
  171.4 30.4 %collective-permute-start.19 = (bf16[2048,256]{1,0:T(8,128)(2,1)}, bf16[2048,256]{1,0:T(8,128)(2,1)}, u32[]{:S(2)}, u32[]{:S(2)}) collective-permute-start(bf16[2048,256]{1,0:T(8,128)(2,1)} %pad_maximum_fusion.2), channel_id=1, source_target_pairs={{0,16},{16,0},{1,17},{17,1},{2,18},{18,2},{3,19},{19,3},{4,20},{20... | collective-permute-start | bytes 3145736 | tf_op jit(solution)/shard_map/ppermute | solution.py:53
  178.2 13.7 %all-to-all-start.4 = ((bf16[4,192,256]{2,1,0:T(8,128)(2,1)}), bf16[4,192,256]{2,1,0:T(8,128)(2,1)}, u32[]{:S(2)}, u32[]{:S(2)}) async-start(bf16[4,192,256]{2,1,0:T(8,128)(2,1)} %pad_maximum_fusion.9), calls=%async_computation.4 | async-start | bytes 786432 | tf_op jit(solution)/shard_map/all_to_all | solution.py:286
  191.8 27.2 %all-to-all-start.5 = ((bf16[8,128,512]{1,2,0:T(8,128)(2,1)}), bf16[8,128,512]{1,2,0:T(8,128)(2,1)S(1)}, u32[]{:S(2)}, u32[]{:S(2)}) async-start(bf16[8,128,512]{1,2,0:T(8,128)(2,1)} %pad_maximum_fusion.1), calls=%async_computation.5 | async-start | bytes 2097152 | tf_op jit(solution)/shard_map/all_to_all | solution.py:22
  219.1 28.1 %all-to-all-start.10 = ((bf16[8,256,256]{2,1,0:T(8,128)(2,1)}), bf16[8,256,256]{2,1,0:T(8,128)(2,1)S(1)}, u32[]{:S(2)}, u32[]{:S(2)}) async-start(bf16[8,256,256]{2,1,0:T(8,128)(2,1)} %bitcast.85), calls=%async_computation.10 | async-start | bytes 2097152 | tf_op jit(solution)/shard_map/all_to_all | solution.py:74
  230.0 7.7 %collective-permute-start.18 = (bf16[1280,256]{1,0:T(8,128)(2,1)}, bf16[1280,256]{1,0:T(8,128)(2,1)}, u32[]{:S(2)}, u32[]{:S(2)}) collective-permute-start(bf16[1280,256]{1,0:T(8,128)(2,1)} %fusion.20), channel_id=1, source_target_pairs={{0,16},{16,0},{1,17},{17,1},{2,18},{18,2},{3,19},{19,3},{4,20},{20... | collective-permute-start | bytes 1966088 | tf_op jit(solution)/shard_map/ppermute | solution.py:53
  247.2 16.7 %all-to-all-start.6 = ((bf16[8,112,256]{2,1,0:T(8,128)(2,1)}), bf16[8,112,256]{2,1,0:T(8,128)(2,1)S(1)}, u32[]{:S(2)}, u32[]{:S(2)}) async-start(bf16[8,112,256]{2,1,0:T(8,128)(2,1)} %bitcast.69), calls=%async_computation.6 | async-start | bytes 917504 | tf_op jit(solution)/shard_map/all_to_all | solution.py:74
  264.7 21.1 %all-to-all-start.8 = ((bf16[8,160,256]{2,1,0:T(8,128)(2,1)}), bf16[8,160,256]{2,1,0:T(8,128)(2,1)S(1)}, u32[]{:S(2)}, u32[]{:S(2)}) async-start(bf16[8,160,256]{2,1,0:T(8,128)(2,1)} %bitcast.232), calls=%async_computation.8 | async-start | bytes 1310720 | tf_op jit(solution)/shard_map/all_to_all | solution.py:74
  287.4 17.0 %all-to-all-start.7 = ((bf16[8,112,256]{2,1,0:T(8,128)(2,1)}), bf16[8,112,256]{2,1,0:T(8,128)(2,1)}, u32[]{:S(2)}, u32[]{:S(2)}) async-start(bf16[8,112,256]{2,1,0:T(8,128)(2,1)} %broadcast_in_dim.47), calls=%async_computation.7 | async-start | bytes 917504 | tf_op jit(solution)/shard_map/all_to_all | solution.py:66
  293.9 15.2 %collective-permute-start.15 = (bf16[256,512]{1,0:T(8,128)(2,1)}, bf16[256,512]{1,0:T(8,128)(2,1)S(1)}, u32[]{:S(2)}, u32[]{:S(2)}) collective-permute-start(bf16[256,512]{1,0:T(8,128)(2,1)} %fusion.16), channel_id=1, source_target_pairs={{0,1},{1,0},{2,3},{3,2},{4,5},{5,4},{6,7},{7,6},{8,9},{9,8},{10,11... | collective-permute-start | bytes 786440 | tf_op jit(solution)/shard_map/ppermute | solution.py:41
  305.5 29.3 %all-to-all-start.11 = ((bf16[8,256,256]{2,1,0:T(8,128)(2,1)}), bf16[8,256,256]{2,1,0:T(8,128)(2,1)S(1)}, u32[]{:S(2)}, u32[]{:S(2)}) async-start(bf16[8,256,256]{2,1,0:T(8,128)(2,1)} %broadcast_in_dim.90), calls=%async_computation.11 | async-start | bytes 2097152 | tf_op jit(solution)/shard_map/all_to_all | solution.py:66
  335.7 21.2 %all-to-all-start.9 = ((bf16[8,160,256]{2,1,0:T(8,128)(2,1)}), bf16[8,160,256]{2,1,0:T(8,128)(2,1)}, u32[]{:S(2)}, u32[]{:S(2)}) async-start(bf16[8,160,256]{2,1,0:T(8,128)(2,1)} %broadcast_in_dim.48), calls=%async_computation.9 | async-start | bytes 1310720 | tf_op jit(solution)/shard_map/all_to_all | solution.py:66
  (72 other events, 858.3 us)
